TPU v7x, 32 devices: a whole 2x2x4 slice. The times are simulated.
32 devices in a mesh: blk: 8 (over z, x), ch: 4 (over y, core).
Axes of the slice: x: 2, y: 2, z: 4, core: 2. Of those that a mesh axis runs over, the one named last changes fastest.
Arguments:
- features: bfloat16 [128, 128, 512], P('blk', 'ch'), may hold values from -6 to 6
- weights: bfloat16 [27, 128, 128], P(None, 'ch'), may hold values from -0.109375 to 0.109375
- bias: float32 [128], P('ch'), may hold values from -3 to 3
- occupancy: int32 [128, 512], P('blk'), may hold values 0 or 1
- live: int32 [8], P('blk'), may hold values from 1 to 16, as said below
- neighbours: int32 [128, 3, 2], replicated, may hold values from 0 to 127, as said below
Outputs:
- convolved: bfloat16 [128, 128, 512], P('blk', 'ch')
Inputs may be any that keep to these rules, and one draw needn't show every extreme that they name: Each device's first live[d] slots are live; some device has all 16 slots live. Along each dimension d, b -> neighbours[b, d, 0] is a one-to-one map of all blocks, and neighbours[b, d, 1] is its inverse. Along each dimension, the upper neighbours of one device's blocks lie on 4 devices, exactly 4 on each.
All inputs are finite; a program needn't handle non-finite values. No bound on the sum of `occupancy` on one device may be relied on, other than what follows from the above.
Results may differ from a plain program's by a relative error of at most 0.003.
Values may be sent and summed in bfloat16 or wider, within the bound.
No kernel may reach another device: no remote copies, remote signals or barrier semaphores. Data moves between devices by JAX's collectives and lax.ppermute only.
A program may use at most 192 MiB of HBM per device.

v0:
```python
import functools

import jax
import jax.numpy as jnp
import numpy as np
from jax import lax
from jax.experimental import pallas as pl
from jax.experimental.pallas import tpu as pltpu
from jax.sharding import PartitionSpec as P

SIDE = 8
PAD = SIDE + 2
LANES = 128
HALF = SIDE * SIDE
VMEM_LIMIT = 56 * 1024 * 1024

FACES = [(1, 0), (1, 1), (2, 0), (2, 1)]
EDGES = [(0, 0), (0, 1), (1, 0), (1, 1)]


def outer(q):
    return PAD - 1 if q == 0 else 0


def inner(q):
    return 1 if q == 0 else SIDE


@functools.lru_cache(None)
def tables():
    expand = np.zeros((LANES, 2 * LANES), np.float32)
    for a in range(2):
        for j in range(SIDE):
            for k in range(SIDE):
                expand[a * HALF + j * SIDE + k, a * LANES + (j + 1) * PAD + k + 1] = 1
    gather = np.zeros((SIDE * LANES, 3 * LANES), np.float32)
    scatter = np.zeros((3 * LANES, SIDE * LANES), np.float32)
    for i in range(SIDE):
        for d, q in FACES:
            for a in range(SIDE):
                lane = (d - 1) * LANES + (1 - q) * HALF + i * SIDE + a
                if d == 1:
                    source, target = outer(q) * PAD + a + 1, inner(q) * PAD + a + 1
                else:
                    source, target = (a + 1) * PAD + outer(q), (a + 1) * PAD + inner(q)
                gather[i * LANES + source, lane] = 1
                scatter[lane, i * LANES + target] = 1
        for e, (qj, qk) in enumerate(EDGES):
            lane = 2 * LANES + e * SIDE + i
            gather[i * LANES + outer(qj) * PAD + outer(qk), lane] = 1
            scatter[lane, i * LANES + inner(qj) * PAD + inner(qk)] = 1
    return expand, gather, scatter


def div(value, size):
    return value >> (size.bit_length() - 1) if size & (size - 1) == 0 else lax.div(value, size)


def mod(value, size):
    return value & (size - 1) if size & (size - 1) == 0 else lax.rem(value, size)


def popcount(x):
    x = x - ((x >> 1) & 0x55555555)
    x = (x & 0x33333333) + ((x >> 2) & 0x33333333)
    x = (x + (x >> 4)) & 0x0F0F0F0F
    x = x + (x >> 8)
    return (x + (x >> 16)) & 0x3F


def clear(ref, size):
    def step(n, _):
        ref[n] = 0
        return 0

    lax.fori_loop(0, size, step, 0)


def slot_of(kind, peer, place, cap, slots):
    rows = 2 * cap + slots // 4
    if kind < 4:
        return peer * rows + (FACES[kind][0] - 1) * cap + place
    if kind < 8:
        return (peer * rows + 2 * cap) * 4 + place
    return peer * cap + place


def table_kernel(peers, cap, slots, me_ref, nbr, send, recv, count, mask):
    me = me_ref[0]
    first = me * slots
    clear(count, 8 * peers)
    clear(mask, 10 * peers)

    def dest(b, kind):
        if kind < 4:
            d, q = FACES[kind]
            return nbr[b * 6 + 2 * d + q]
        qj, qk = EDGES[kind - 4]
        return nbr[nbr[b * 6 + 2 + qj] * 6 + 4 + qk]

    def source(r, kind):
        if kind >= 8:
            return nbr[r * 6 + 1 - (kind - 8)]
        if kind < 4:
            d, q = FACES[kind]
            return nbr[r * 6 + 2 * d + 1 - q]
        qj, qk = EDGES[kind - 4]
        return nbr[nbr[r * 6 + 4 + 1 - qk] * 6 + 2 + 1 - qj]

    def gather(s, _):
        for kind in range(8):
            peer = div(dest(first + s, kind), slots)
            place = count[kind * peers + peer]
            count[kind * peers + peer] = place + 1
            send[kind * slots + s] = slot_of(kind, peer, place, cap, slots)
        for kind in range(10):
            b = source(first + s, kind)
            at = kind * peers + div(b, slots)
            mask[at] = mask[at] | (1 << mod(b, slots))
        return 0

    lax.fori_loop(0, slots, gather, 0)

    def rank(r, _):
        for kind in range(10):
            b = source(first + r, kind)
            peer = div(b, slots)
            before = popcount(mask[kind * peers + peer] & ((1 << mod(b, slots)) - 1))
            recv[kind * slots + r] = slot_of(kind, peer, before, cap, slots)
        return 0

    lax.fori_loop(0, slots, rank, 0)


def active_row(occ_ref, s, live):
    return occ_ref[pl.ds(s, 1), :].astype(jnp.float32) * (s < live).astype(jnp.float32)


def pack_kernel(peers, cap, slots, me_ref, live_ref, nbr, occ, low, high, out, count):
    first = me_ref[0] * slots
    live = live_ref[0]
    clear(count, 2 * peers)
    for s in range(slots):
        row = active_row(occ, s, live).astype(jnp.bfloat16)
        for q in range(2):
            peer = div(nbr[(first + s) * 6 + q], slots)
            place = count[q * peers + peer]
            count[q * peers + peer] = place + 1
            half = slice(0, HALF) if q == 1 else slice(HALF, LANES)
            face = low if q == 1 else high
            lanes = row[:, :LANES] if q == 1 else row[:, -LANES:]
            out[peer * cap + place, :, half] = (face[s] * lanes)[:, half]


def order_kernel(slots, recv, arrived, out):
    lane = lax.broadcasted_iota(jnp.int32, arrived.shape[1:], 1)
    for r in range(slots):
        up = arrived[recv[8 * slots + r]]
        down = arrived[recv[9 * slots + r]]
        out[r] = jnp.where(lane < HALF, down, up)


def conv_kernel(
    keys, slots, cap, group, me_ref, live_ref, send, occ, weights, expand, gather, *refs
):
    n = len(keys)
    xs, hs = refs[:n], refs[n : 2 * n]
    out, faces = refs[2 * n : 2 * n + 2]
    wide, rows, stack, prod, packed = refs[2 * n + 2 :]
    channels = weights.shape[1]
    every = weights.shape[2]
    step = pl.program_id(0)
    me = me_ref[0]
    live = live_ref[0]

    @pl.when(step == 0)
    def _():
        for g in range(9):
            for r in range(3):
                wide[g * channels : (g + 1) * channels, r * every : (r + 1) * every] = weights[3 * g + r]

    def block(b, _):
        s = step * group + b
        row = active_row(occ, s, live).astype(jnp.bfloat16)
        for key, x, h in zip(keys, xs, hs):
            at = pl.multiple_of((me ^ key) * channels, channels)
            masked = x[b] * row
            for v in range(4):
                rows[v, pl.ds(at, channels), :] = masked[:, v * LANES : (v + 1) * LANES]
            rows[4, pl.ds(at, channels), :] = h[b]
        for v in range(5):
            planes = jnp.dot(rows[v], expand[...], preferred_element_type=jnp.float32)
            for a in range(2):
                layer = 2 * v + 1 + a if v < 4 else 9 * (1 - a)
                at = slice(layer * LANES, (layer + 1) * LANES)
                plane = planes[:, a * LANES : (a + 1) * LANES]
                stack[0:every, at] = pltpu.roll(plane, 1, axis=1).astype(jnp.bfloat16)
                stack[every : 2 * every, at] = plane.astype(jnp.bfloat16)
                stack[2 * every : 3 * every, at] = pltpu.roll(plane, LANES - 1, axis=1).astype(jnp.bfloat16)
        prod[...] = jnp.dot(wide[...], stack[...], preferred_element_type=jnp.float32)
        for layer in range(SIDE):
            at = slice(layer * LANES, (layer + 1) * LANES)
            sums = []
            for q in range(3):
                total = None
                for p in range(3):
                    first = (3 * p + q) * channels
                    part = prod[first : first + channels, (layer + p) * LANES : (layer + p + 1) * LANES]
                    total = part if total is None else total + part
                sums.append(total)
            result = sums[1] + pltpu.roll(sums[0], PAD, axis=1) + pltpu.roll(sums[2], LANES - PAD, axis=1)
            out[b, :, at] = result
            packed[b, :, at] = result.astype(jnp.bfloat16)

        return 0

    lax.fori_loop(0, group, block, 0)
    shell = jnp.dot(
        packed[...].reshape(group * channels, SIDE * LANES), gather[...], preferred_element_type=jnp.float32
    )
    lane = lax.broadcasted_iota(jnp.int32, (channels, LANES), 1)
    for b in range(group):
        s = step * group + b
        mine = shell[b * channels : (b + 1) * channels]
        for d in range(2):
            pair = mine[:, d * LANES : (d + 1) * LANES].astype(jnp.bfloat16)
            faces[send[(2 * d + 1) * slots + s], :, :HALF] = pair[:, :HALF]
            faces[send[2 * d * slots + s], :, HALF:] = pair[:, HALF:]
        edge = mine[:, 2 * LANES :]
        for e in range(4):
            slot = send[(4 + e) * slots + s]
            shift = (slot & 3) * 32
            moved = pltpu.roll(edge, shift, axis=1).astype(jnp.bfloat16)
            keep = jnp.logical_and(lane >= shift + e * SIDE, lane < shift + (e + 1) * SIDE)
            faces[slot >> 2] = jnp.where(keep, moved, faces[slot >> 2])


def final_kernel(slots, recv, live_ref, occ, bias, scatter, squeeze, base, faces, out, shell):
    channels = base.shape[1]
    live = live_ref[0]
    lane = lax.broadcasted_iota(jnp.int32, (channels, LANES), 1)
    for r in range(slots):
        for d in range(2):
            up = faces[recv[2 * d * slots + r]]
            down = faces[recv[(2 * d + 1) * slots + r]]
            shell[r, :, d * LANES : (d + 1) * LANES] = jnp.where(lane < HALF, down, up)
        total = jnp.zeros((channels, LANES), jnp.float32)
        for e in range(4):
            slot = recv[(4 + e) * slots + r]
            moved = pltpu.roll(faces[slot >> 2].astype(jnp.float32), (LANES - (slot & 3) * 32) & (LANES - 1), axis=1)
            keep = jnp.logical_and(lane >= e * SIDE, lane < (e + 1) * SIDE)
            total = jnp.where(keep, moved, total)
        shell[r, :, 2 * LANES :] = total.astype(jnp.bfloat16)
    added = jnp.dot(
        shell[...].reshape(slots * channels, 3 * LANES), scatter[...], preferred_element_type=jnp.float32
    )
    for r in range(slots):
        summed = base[r] + added[r * channels : (r + 1) * channels] + bias[...]
        rounded = summed.astype(jnp.bfloat16)
        row = active_row(occ, r, live).astype(jnp.bfloat16)
        for v in range(4):
            pair = rounded[:, 2 * v * LANES : 2 * (v + 1) * LANES]
            at = slice(v * LANES, (v + 1) * LANES)
            flat = jnp.dot(pair, squeeze[...], preferred_element_type=jnp.float32).astype(jnp.bfloat16)
            out[r, :, at] = flat * row[:, at]


def spread(x, axis, size):
    have = {0: x}
    bit = size >> 1
    while bit:
        for key in list(have):
            have[key ^ bit] = lax.ppermute(have[key], axis, [(n, n ^ bit) for n in range(size)])
        bit >>= 1
    return have


def shards(features, weights, bias, occupancy, live, neighbours):
    slots, channels, voxels = features.shape
    peers = lax.axis_size("blk")
    members = lax.axis_size("ch")
    cap = max(2, 2 * slots // peers)
    every = channels * members
    group = 4
    bf16, f32, i32 = jnp.bfloat16, jnp.float32, jnp.int32
    smem = pl.BlockSpec(memory_space=pltpu.SMEM)
    vmem = pl.BlockSpec(memory_space=pltpu.VMEM)
    params = pltpu.CompilerParams(vmem_limit_bytes=VMEM_LIMIT)
    expand, gather, scatter = (jnp.asarray(t, bf16) for t in tables())
    squeeze = expand.T
    place = lax.axis_index("blk").astype(i32).reshape(1)
    member = lax.axis_index("ch").astype(i32).reshape(1)
    nbr = neighbours.reshape(-1)

    have = spread(features, "ch", members)

    corner = pl.BlockSpec((slots, channels, LANES), lambda n: (0, 0, 0))
    corner_last = pl.BlockSpec((slots, channels, LANES), lambda n: (0, 0, voxels // LANES - 1))
    outgoing = pl.pallas_call(
        functools.partial(pack_kernel, peers, cap, slots),
        grid=(1,),
        out_shape=jax.ShapeDtypeStruct((peers * cap, channels, LANES), bf16),
        in_specs=[smem, smem, smem, vmem, corner, corner_last],
        out_specs=vmem,
        scratch_shapes=[pltpu.SMEM((2 * peers,), i32)],
        compiler_params=params,
        name="pack_layers",
    )(place, live, nbr, occupancy, features, features)
    arrived = lax.all_to_all(outgoing, "blk", split_axis=0, concat_axis=0, tiled=True)

    send, recv = pl.pallas_call(
        functools.partial(table_kernel, peers, cap, slots),
        out_shape=(jax.ShapeDtypeStruct((8 * slots,), i32), jax.ShapeDtypeStruct((10 * slots,), i32)),
        in_specs=[smem, smem],
        out_specs=(smem, smem),
        scratch_shapes=[pltpu.SMEM((8 * peers,), i32), pltpu.SMEM((10 * peers,), i32)],
        name="slot_tables",
    )(place, nbr)

    layers = pl.pallas_call(
        functools.partial(order_kernel, slots),
        out_shape=jax.ShapeDtypeStruct((slots, channels, LANES), bf16),
        in_specs=[smem, vmem],
        out_specs=vmem,
        compiler_params=params,
        name="order_layers",
    )(recv, arrived)
    halo = spread(layers, "ch", members)

    keys = sorted(have)
    own = pl.BlockSpec((group, channels, voxels), lambda n: (n, 0, 0))
    own_halo = pl.BlockSpec((group, channels, LANES), lambda n: (n, 0, 0))
    base, faces = pl.pallas_call(
        functools.partial(conv_kernel, keys, slots, cap, group),
        grid=(slots // group,),
        out_shape=(
            jax.ShapeDtypeStruct((slots, channels, SIDE * LANES), f32),
            jax.ShapeDtypeStruct((peers * (2 * cap + slots // 4), channels, LANES), bf16),
        ),
        in_specs=[smem, smem, smem, vmem, vmem, vmem, vmem] + [own] * len(keys) + [own_halo] * len(keys),
        out_specs=(pl.BlockSpec((group, channels, SIDE * LANES), lambda n: (n, 0, 0)), vmem),
        scratch_shapes=[
            pltpu.VMEM((9 * channels, 3 * every), bf16),
            pltpu.VMEM((5, every, LANES), bf16),
            pltpu.VMEM((3 * every, PAD * LANES), bf16),
            pltpu.VMEM((9 * channels, PAD * LANES), f32),
            pltpu.VMEM((group, channels, SIDE * LANES), bf16),
        ],
        compiler_params=params,
        name="convolve",
    )(member, live, send, occupancy, weights, expand, gather, *[have[k] for k in keys], *[halo[k] for k in keys])

    faces = lax.all_to_all(faces, "blk", split_axis=0, concat_axis=0, tiled=True)

    return pl.pallas_call(
        functools.partial(final_kernel, slots),
        out_shape=jax.ShapeDtypeStruct((slots, channels, voxels), bf16),
        in_specs=[smem, smem] + [vmem] * 6,
        out_specs=vmem,
        scratch_shapes=[pltpu.VMEM((slots, channels, 3 * LANES), bf16)],
        compiler_params=params,
        name="finish",
    )(recv, live, occupancy, bias[:, None], scatter, squeeze, base, faces)


def solution(mesh):
    in_specs = (P("blk", "ch", None), P(None, "ch", None), P("ch"), P("blk", None), P("blk"), P())
    out_specs = P("blk", "ch", None)
    return jax.shard_map(shards, mesh=mesh, in_specs=in_specs, out_specs=out_specs, check_vma=False)
```

profile of v0, /device:TPU:0, one launch (start us, length us, event | category | flops | bytes accessed | tf_op | source)
XLA Modules:
  0.0 82.7 jit_solution(16107670055091015117)
XLA Ops:
  0.0 0.0 copy-start
  0.0 3.0 %collective-permute-start.1 = (bf16[16,32,512]{2,1,0:T(8,128)(2,1)}, bf16[16,32,512]{2,1,0:T(8,128)(2,1)S(1)}, u32[]{:S(2)}, u32[]{:S(2)}) collective-permute-start(bf16[16,32,512]{2,1,0:T(8,128)(2,1)} %refs_0_.1), channel_id=1, source_target_pairs={{0,2},{1,3},{2,0},{3,1},{4,6},{5,7},{6,4},{7,5},{8,10},{9,11},{10,... | collective-permute-start | bytes 1572872 | tf_op jit(solution)/shard_map/ppermute | solution.py:273
  3.6 0.8 %copy.11 = s32[128,3,2]{2,1,0:T(4,128)S(1)} copy(s32[128,3,2]{0,2,1:T(2,128)} %param.14) | data formatting | bytes 6144 | tf_op args[5]
  4.5 0.8 reshape.10.nbr
  5.3 2.0 %pack_layers.1 = bf16[32,32,128]{2,1,0:T(8,128)(2,1)} custom-call(s32[1]{0:T(128)} %bitcast.me_ref, s32[1]{0:T(128)S(6)} %copy.13.live_ref, s32[768]{0:T(1024)} %reshape.10.nbr, s32[16,512]{1,0:T(8,128)} %occ.5, bf16[16,32,512]{2,1,0:T(8,128)(2,1)} %refs_0_.1, bf16[16,32,512]{2,1,0:T(8,128)(2,1)} %refs_0_.1), custom_call_target="tpu_custom_call" | custom-call | tf_op jit(solution)/shard_map/pack_layers/pallas_call | solution.py:299
  7.2 5.8 %all-to-all-start = ((bf16[32,32,128]{2,1,0:T(8,128)(2,1)}), bf16[32,32,128]{2,1,0:T(8,128)(2,1)S(1)}, u32[]{:S(2)}, u32[]{:S(2)}) async-start(bf16[32,32,128]{2,1,0:T(8,128)(2,1)} %pack_layers.1), calls=%async_computation | async-start | bytes 524288 | tf_op jit(solution)/shard_map/all_to_all | solution.py:309
  13.0 0.0 copy-done
  13.0 0.1 collective-permute-start
  13.1 2.1 %collective-permute-done.1.refs_2_ = bf16[16,32,512]{2,1,0:T(8,128)(2,1)S(1)} collective-permute-done((bf16[16,32,512]{2,1,0:T(8,128)(2,1)}, bf16[16,32,512]{2,1,0:T(8,128)(2,1)S(1)}, u32[]{:S(2)}, u32[]{:S(2)}) %collective-permute-start.1) | collective-permute-done | bytes 524320 | tf_op jit(solution)/shard_map/ppermute | solution.py:273
  15.2 0.0 copy-start.3
  15.2 0.0 collective-permute-start.2
  15.2 4.9 %slot_tables.1 = (s32[128]{0:T(128)}, s32[160]{0:T(256)}) custom-call(s32[1]{0:T(128)} %bitcast.me_ref, s32[768]{0:T(1024)} %reshape.10.nbr), custom_call_target="tpu_custom_call" | custom-call | tf_op jit(solution)/shard_map/slot_tables/pallas_call | solution.py:311
  20.1 1.6 %all-to-all-done.arrived = bf16[32,32,128]{2,1,0:T(8,128)(2,1)S(1)} async-done(((bf16[32,32,128]{2,1,0:T(8,128)(2,1)}), bf16[32,32,128]{2,1,0:T(8,128)(2,1)S(1)}, u32[]{:S(2)}, u32[]{:S(2)}) %all-to-all-start) | async-done | bytes 262176 | tf_op jit(solution)/shard_map/all_to_all | solution.py:309
  21.7 0.0 copy-start.2
  21.7 0.7 copy-done.2
  22.4 1.6 %order_layers.1.refs_4_ = bf16[16,32,128]{2,1,0:T(8,128)(2,1)} custom-call(s32[160]{0:T(256)} %get-tuple-element.9.recv, bf16[32,32,128]{2,1,0:T(8,128)(2,1)} %copy-done.2), custom_call_target="tpu_custom_call" | custom-call | tf_op jit(solution)/shard_map/order_layers/pallas_call | solution.py:320
  24.0 0.5 collective-permute-start.4
  24.5 0.0 collective-permute-start.3
  24.5 4.7 %collective-permute-done.4.refs_6_ = bf16[16,32,128]{2,1,0:T(8,128)(2,1)S(1)} collective-permute-done((bf16[16,32,128]{2,1,0:T(8,128)(2,1)}, bf16[16,32,128]{2,1,0:T(8,128)(2,1)S(1)}, u32[]{:S(2)}, u32[]{:S(2)}) %collective-permute-start.4) | collective-permute-done | bytes 131104 | tf_op jit(solution)/shard_map/ppermute | solution.py:273
  29.2 0.0 copy-start.6
  29.2 0.0 collective-permute-start.5
  29.2 0.0 collective-permute-done.refs_1_
  29.2 0.0 copy-start.4
  29.2 0.0 collective-permute-done.3.refs_5_
  29.2 0.0 copy-start.7
  29.2 1.3 %collective-permute-done.5.refs_7_ = bf16[16,32,128]{2,1,0:T(8,128)(2,1)S(1)} collective-permute-done((bf16[16,32,128]{2,1,0:T(8,128)(2,1)S(1)}, bf16[16,32,128]{2,1,0:T(8,128)(2,1)S(1)}, u32[]{:S(2)}, u32[]{:S(2)}) %collective-permute-start.5) | collective-permute-done | bytes 131104 | tf_op jit(solution)/shard_map/ppermute | solution.py:273
  30.6 0.0 copy-start.8
  30.6 0.0 collective-permute-done.2.refs_3_
  30.6 0.0 copy-start.5
  30.6 0.0 copy-done.3
  30.6 0.0 copy-done.6
  30.6 0.0 copy-done.4
  30.6 0.0 copy-done.7
  30.6 0.6 copy-done.8
  31.2 0.2 copy-done.5
  31.4 0.0 copy-start.9
  31.4 20.4 %convolve.1 = (f32[16,32,1024]{2,1,0:T(8,128)}, bf16[96,32,128]{2,1,0:T(8,128)(2,1)}) custom-call(s32[1]{0:T(128)} %bitcast.2.me_ref, s32[1]{0:T(128)S(6)} %copy.13.live_ref, s32[128]{0:T(128)} %get-tuple-element.10.send, s32[16,512]{1,0:T(8,128)} %occ.5, bf16[27,32,128]{2,1,0:T(8,128)(2,1)} %weights.1, bf16[128,256]{1,0:T(8,128)(2,1)} %constant.15.clone.expand, ...), custom_call_target="tpu_custom_call" | custom-call | tf_op jit(solution)/shard_map/convolve/pallas_call | solution.py:333
  51.8 5.3 %all-to-all-start.1 = ((bf16[96,32,128]{2,1,0:T(8,128)(2,1)}), bf16[96,32,128]{2,1,0:T(8,128)(2,1)S(1)}, u32[]{:S(2)}, u32[]{:S(2)}) async-start(bf16[96,32,128]{2,1,0:T(8,128)(2,1)} %get-tuple-element.12), calls=%async_computation.1 | async-start | bytes 1572864 | tf_op jit(solution)/shard_map/all_to_all | solution.py:353
  57.2 0.0 copy-done.9
  57.2 0.7 copy.12.bias
  57.9 19.8 %all-to-all-done.1.faces = bf16[96,32,128]{2,1,0:T(8,128)(2,1)S(1)} async-done(((bf16[96,32,128]{2,1,0:T(8,128)(2,1)}), bf16[96,32,128]{2,1,0:T(8,128)(2,1)S(1)}, u32[]{:S(2)}, u32[]{:S(2)}) %all-to-all-start.1) | async-done | bytes 786464 | tf_op jit(solution)/shard_map/all_to_all | solution.py:353
  77.7 0.0 copy-start.1
  77.7 0.9 %copy-done.1 = bf16[96,32,128]{2,1,0:T(8,128)(2,1)} copy-done((bf16[96,32,128]{2,1,0:T(8,128)(2,1)}, bf16[96,32,128]{2,1,0:T(8,128)(2,1)S(1)}, u32[]{:S(2)}) %copy-start.1) | copy-done | bytes 786456
  78.5 4.2 %finish.1 = bf16[16,32,512]{2,1,0:T(8,128)(2,1)} custom-call(s32[160]{0:T(256)} %get-tuple-element.9.recv, s32[1]{0:T(128)S(6)} %copy.13.live_ref, s32[16,512]{1,0:T(8,128)} %occ.5, f32[32,1]{1,0:T(8,128)} %copy.12.bias, bf16[384,1024]{1,0:T(8,128)(2,1)} %constant.17.clone.scatter, bf16[256,128]{1,0:T(8,128)(2,1)} %constant.19.squeeze, ...), custom_call_target="tpu_custom_call" | custom-call | tf_op jit(solution)/shard_map/finish/pallas_call | solution.py:355
Async XLA Ops:
  0.0 13.0 %copy-start = (bf16[16,32,512]{2,1,0:T(8,128)(2,1)S(1)}, bf16[16,32,512]{2,1,0:T(8,128)(2,1)}, u32[]{:S(2)}) copy-start(bf16[16,32,512]{2,1,0:T(8,128)(2,1)} %refs_0_.1) | copy-start | bytes 1572868
  0.0 15.2 %collective-permute-start.1 = (bf16[16,32,512]{2,1,0:T(8,128)(2,1)}, bf16[16,32,512]{2,1,0:T(8,128)(2,1)S(1)}, u32[]{:S(2)}, u32[]{:S(2)}) collective-permute-start(bf16[16,32,512]{2,1,0:T(8,128)(2,1)} %refs_0_.1), channel_id=1, source_target_pairs={{0,2},{1,3},{2,0},{3,1},{4,6},{5,7},{6,4},{7,5},{8,10},{9,11},{10,... | collective-permute-start | bytes 1572872 | tf_op jit(solution)/shard_map/ppermute | solution.py:273
  7.2 14.4 %all-to-all-start = ((bf16[32,32,128]{2,1,0:T(8,128)(2,1)}), bf16[32,32,128]{2,1,0:T(8,128)(2,1)S(1)}, u32[]{:S(2)}, u32[]{:S(2)}) async-start(bf16[32,32,128]{2,1,0:T(8,128)(2,1)} %pack_layers.1), calls=%async_computation | async-start | bytes 524288 | tf_op jit(solution)/shard_map/all_to_all | solution.py:309
  13.0 16.2 %collective-permute-start = (bf16[16,32,512]{2,1,0:T(8,128)(2,1)S(1)}, bf16[16,32,512]{2,1,0:T(8,128)(2,1)S(1)}, u32[]{:S(2)}, u32[]{:S(2)}) collective-permute-start(bf16[16,32,512]{2,1,0:T(8,128)(2,1)S(1)} %copy-done), channel_id=1, source_target_pairs={{0,1},{1,0},{2,3},{3,2},{4,5},{5,4},{6,7},{7,6},{8,9},{9,8},{10,11... | collective-permute-start | bytes 1572872 | tf_op jit(solution)/shard_map/ppermute | solution.py:273
  15.2 15.4 %copy-start.3 = (bf16[16,32,512]{2,1,0:T(8,128)(2,1)}, bf16[16,32,512]{2,1,0:T(8,128)(2,1)S(1)}, u32[]{:S(2)}) copy-start(bf16[16,32,512]{2,1,0:T(8,128)(2,1)S(1)} %collective-permute-done.1.refs_2_) | copy-start | bytes 1572868
  15.2 15.4 %collective-permute-start.2 = (bf16[16,32,512]{2,1,0:T(8,128)(2,1)S(1)}, bf16[16,32,512]{2,1,0:T(8,128)(2,1)S(1)}, u32[]{:S(2)}, u32[]{:S(2)}) collective-permute-start(bf16[16,32,512]{2,1,0:T(8,128)(2,1)S(1)} %collective-permute-done.1.refs_2_), channel_id=1, source_target_pairs={{0,1},{1,0},{2,3},{3,2},{4,5},{5,4},{6,7},{7,6},{8,9},{9,8},{10,11... | collective-permute-start | bytes 1572872 | tf_op jit(solution)/shard_map/ppermute | solution.py:273
  21.7 0.7 copy-start.2
  24.0 5.2 %collective-permute-start.4 = (bf16[16,32,128]{2,1,0:T(8,128)(2,1)}, bf16[16,32,128]{2,1,0:T(8,128)(2,1)S(1)}, u32[]{:S(2)}, u32[]{:S(2)}) collective-permute-start(bf16[16,32,128]{2,1,0:T(8,128)(2,1)} %order_layers.1.refs_4_), channel_id=1, source_target_pairs={{0,2},{1,3},{2,0},{3,1},{4,6},{5,7},{6,4},{7,5},{8,10},{9,11},{10,... | collective-permute-start | bytes 393224 | tf_op jit(solution)/shard_map/ppermute | solution.py:273
  24.5 4.7 %collective-permute-start.3 = (bf16[16,32,128]{2,1,0:T(8,128)(2,1)}, bf16[16,32,128]{2,1,0:T(8,128)(2,1)S(1)}, u32[]{:S(2)}, u32[]{:S(2)}) collective-permute-start(bf16[16,32,128]{2,1,0:T(8,128)(2,1)} %order_layers.1.refs_4_), channel_id=1, source_target_pairs={{0,1},{1,0},{2,3},{3,2},{4,5},{5,4},{6,7},{7,6},{8,9},{9,8},{10,11... | collective-permute-start | bytes 393224 | tf_op jit(solution)/shard_map/ppermute | solution.py:273
  29.2 1.4 %copy-start.6 = (bf16[16,32,128]{2,1,0:T(8,128)(2,1)}, bf16[16,32,128]{2,1,0:T(8,128)(2,1)S(1)}, u32[]{:S(2)}) copy-start(bf16[16,32,128]{2,1,0:T(8,128)(2,1)S(1)} %collective-permute-done.4.refs_6_) | copy-start | bytes 393220
  29.2 1.3 %collective-permute-start.5 = (bf16[16,32,128]{2,1,0:T(8,128)(2,1)S(1)}, bf16[16,32,128]{2,1,0:T(8,128)(2,1)S(1)}, u32[]{:S(2)}, u32[]{:S(2)}) collective-permute-start(bf16[16,32,128]{2,1,0:T(8,128)(2,1)S(1)} %collective-permute-done.4.refs_6_), channel_id=1, source_target_pairs={{0,1},{1,0},{2,3},{3,2},{4,5},{5,4},{6,7},{7,6},{8,9},{9,8},{10,11... | collective-permute-start | bytes 393224 | tf_op jit(solution)/shard_map/ppermute | solution.py:273
  29.2 1.4 %copy-start.4 = (bf16[16,32,512]{2,1,0:T(8,128)(2,1)}, bf16[16,32,512]{2,1,0:T(8,128)(2,1)S(1)}, u32[]{:S(2)}) copy-start(bf16[16,32,512]{2,1,0:T(8,128)(2,1)S(1)} %collective-permute-done.refs_1_) | copy-start | bytes 1572868
  29.2 1.4 %copy-start.7 = (bf16[16,32,128]{2,1,0:T(8,128)(2,1)}, bf16[16,32,128]{2,1,0:T(8,128)(2,1)S(1)}, u32[]{:S(2)}) copy-start(bf16[16,32,128]{2,1,0:T(8,128)(2,1)S(1)} %collective-permute-done.3.refs_5_) | copy-start | bytes 393220
  30.6 0.7 copy-start.8
  30.6 0.9 %copy-start.5 = (bf16[16,32,512]{2,1,0:T(8,128)(2,1)}, bf16[16,32,512]{2,1,0:T(8,128)(2,1)S(1)}, u32[]{:S(2)}) copy-start(bf16[16,32,512]{2,1,0:T(8,128)(2,1)S(1)} %collective-permute-done.2.refs_3_) | copy-start | bytes 1572868
  31.4 25.8 %copy-start.9 = (f32[32]{0:T(128)S(1)}, f32[32]{0:T(128)}, u32[]{:S(2)}) copy-start(f32[32]{0:T(128)} %param.11) | copy-start | bytes 388
  51.8 25.8 %all-to-all-start.1 = ((bf16[96,32,128]{2,1,0:T(8,128)(2,1)}), bf16[96,32,128]{2,1,0:T(8,128)(2,1)S(1)}, u32[]{:S(2)}, u32[]{:S(2)}) async-start(bf16[96,32,128]{2,1,0:T(8,128)(2,1)} %get-tuple-element.12), calls=%async_computation.1 | async-start | bytes 1572864 | tf_op jit(solution)/shard_map/all_to_all | solution.py:353
  77.7 0.9 %copy-start.1 = (bf16[96,32,128]{2,1,0:T(8,128)(2,1)}, bf16[96,32,128]{2,1,0:T(8,128)(2,1)S(1)}, u32[]{:S(2)}) copy-start(bf16[96,32,128]{2,1,0:T(8,128)(2,1)S(1)} %all-to-all-done.1.faces) | copy-start | bytes 2359300
where the time goes:
time: 83.2 us; the launch traced here: 82.7 us
  Pallas kernels  33.1 us (40%)
  waiting for transfers between devices  29.4 us (35%)
  starting transfers between devices  14.7 us (18%)
  local copies, waits for them, and re-layouts  4.74 us (6%)
    pallas_call x1, Pallas kernels, shards(): pl.pallas_call(functools.partial(conv_kernel, keys, slots, cap, group), g...  20.4 us
    all_to_all x1, waiting for transfers between devices, shards(): lax.all_to_all(faces, 'blk', split_axis=0, concat_axis=0, tiled=True)  19.8 us
    ppermute x6, waiting for transfers between devices, spread(): lax.ppermute(have[key], axis, [(n, n ^ bit) for n in range(size)])  8.06 us
    all_to_all x1, starting transfers between devices, shards(): lax.all_to_all(outgoing, 'blk', split_axis=0, concat_axis=0, tiled=True)  5.81 us
    all_to_all x1, starting transfers between devices, shards(): lax.all_to_all(faces, 'blk', split_axis=0, concat_axis=0, tiled=True)  5.35 us
    pallas_call x1, Pallas kernels, shards(): pl.pallas_call(functools.partial(table_kernel, peers, cap, slots), out_sh...  4.88 us
    pallas_call x1, Pallas kernels, shards(): pl.pallas_call(functools.partial(final_kernel, slots), out_shape=jax.Shap...  4.21 us
    ppermute x6, starting transfers between devices, spread(): lax.ppermute(have[key], axis, [(n, n ^ bit) for n in range(size)])  3.58 us
  transfers between devices with their start and end apart: 8, of which 5 were waited for; matrix products, arithmetic and copies ran while one was open for 3% of the time, Pallas kernels for 10%

commit v1 on v0

v1 whole, which is shorter than its diff:
```python
import functools

import jax
import jax.numpy as jnp
import numpy as np
from jax import lax
from jax.experimental import pallas as pl
from jax.experimental.pallas import tpu as pltpu
from jax.sharding import PartitionSpec as P

SIDE = 8
PAD = SIDE + 2
LANES = 128
HALF = SIDE * SIDE
VMEM_LIMIT = 57 * 1024 * 1024

FACES = [(1, 0), (1, 1), (2, 0), (2, 1)]
EDGES = [(0, 0), (0, 1), (1, 0), (1, 1)]


def outer(q):
    return PAD - 1 if q == 0 else 0


def inner(q):
    return 0 if q == 0 else SIDE - 1


@functools.lru_cache(None)
def tables():
    expand = np.zeros((LANES, 2 * LANES), np.float32)
    for a in range(2):
        for j in range(SIDE):
            for k in range(SIDE):
                expand[a * HALF + j * SIDE + k, a * LANES + (j + 1) * PAD + k + 1] = 1
    gather = np.zeros((SIDE * LANES, 3 * LANES), np.float32)
    scatter = np.zeros((3 * LANES, SIDE * HALF), np.float32)
    for i in range(SIDE):
        for d, q in FACES:
            for a in range(SIDE):
                lane = (d - 1) * LANES + (1 - q) * HALF + i * SIDE + a
                if d == 1:
                    source, target = outer(q) * PAD + a + 1, inner(q) * SIDE + a
                else:
                    source, target = (a + 1) * PAD + outer(q), a * SIDE + inner(q)
                gather[i * LANES + source, lane] = 1
                scatter[lane, i * HALF + target] = 1
        for quarter in range(4):
            for e, (qj, qk) in enumerate(EDGES):
                lane = 2 * LANES + quarter * 4 * SIDE + e * SIDE + i
                gather[i * LANES + outer(qj) * PAD + outer(qk), lane] = 1
                scatter[lane, i * HALF + inner(qj) * SIDE + inner(qk)] = 1
    return expand, gather, scatter


def div(value, size):
    return value >> (size.bit_length() - 1) if size & (size - 1) == 0 else lax.div(value, size)


def mod(value, size):
    return value & (size - 1) if size & (size - 1) == 0 else lax.rem(value, size)


def popcount(x):
    x = x - ((x >> 1) & 0x55555555)
    x = (x & 0x33333333) + ((x >> 2) & 0x33333333)
    x = (x + (x >> 4)) & 0x0F0F0F0F
    x = x + (x >> 8)
    return (x + (x >> 16)) & 0x3F


def clear(ref, size):
    def step(n, _):
        ref[n] = 0
        return 0

    lax.fori_loop(0, size, step, 0)


def slot_of(kind, peer, place, cap, slots):
    rows = 2 * cap + slots // 4
    if kind < 4:
        return peer * rows + (FACES[kind][0] - 1) * cap + place
    if kind < 8:
        return (peer * rows + 2 * cap) * 4 + place
    return peer * cap + place


def neighbour(nbr, b, d, q):
    return nbr[d, q, b]


def dest(nbr, b, kind):
    if kind < 4:
        return neighbour(nbr, b, *FACES[kind])
    qj, qk = EDGES[kind - 4]
    return neighbour(nbr, neighbour(nbr, b, 1, qj), 2, qk)


def source(nbr, r, kind):
    if kind >= 8:
        return neighbour(nbr, r, 0, 1 - (kind - 8))
    if kind < 4:
        d, q = FACES[kind]
        return neighbour(nbr, r, d, 1 - q)
    qj, qk = EDGES[kind - 4]
    return neighbour(nbr, neighbour(nbr, r, 2, 1 - qk), 1, 1 - qj)


def send_kernel(peers, cap, slots, me_ref, nbr, send, count):
    first = me_ref[0] * slots
    clear(count, 8 * peers)

    def place_of(s, _):
        for kind in range(8):
            peer = div(dest(nbr, first + s, kind), slots)
            place = count[kind * peers + peer]
            count[kind * peers + peer] = place + 1
            send[kind * slots + s] = slot_of(kind, peer, place, cap, slots) if kind < 4 else peer * slots + place
        return 0

    lax.fori_loop(0, slots, place_of, 0)


def table_kernel(kinds, peers, cap, slots, me_ref, nbr, recv, mask):
    first = me_ref[0] * slots
    clear(mask, len(kinds) * peers)

    def gather(s, _):
        for n, kind in enumerate(kinds):
            b = source(nbr, first + s, kind)
            at = n * peers + div(b, slots)
            mask[at] = mask[at] | (1 << mod(b, slots))
        return 0

    lax.fori_loop(0, slots, gather, 0)

    def rank(r, _):
        for n, kind in enumerate(kinds):
            b = source(nbr, first + r, kind)
            peer = div(b, slots)
            before = popcount(mask[n * peers + peer] & ((1 << mod(b, slots)) - 1))
            recv[n * slots + r] = slot_of(kind, peer, before, cap, slots)
        return 0

    lax.fori_loop(0, slots, rank, 0)


def early_kernel(peers, cap, slots, me_ref, nbr, send, recv, count, mask):
    send_kernel(peers, cap, slots, me_ref, nbr, send, count)
    table_kernel((8, 9), peers, cap, slots, me_ref, nbr, recv, mask)


def active_row(occ_ref, s, live):
    return occ_ref[pl.ds(s, 1), :].astype(jnp.float32) * (s < live).astype(jnp.float32)


def pack_kernel(peers, cap, slots, me_ref, live_ref, nbr, occ, low, high, out, count):
    first = me_ref[0] * slots
    live = live_ref[0]
    clear(count, 2 * peers)
    for s in range(slots):
        row = active_row(occ, s, live).astype(jnp.bfloat16)
        for q in range(2):
            peer = div(neighbour(nbr, first + s, 0, q), slots)
            place = count[q * peers + peer]
            count[q * peers + peer] = place + 1
            half = slice(0, HALF) if q == 1 else slice(HALF, LANES)
            face = low if q == 1 else high
            lanes = row[:, :LANES] if q == 1 else row[:, -LANES:]
            out[peer * cap + place, :, half] = (face[s] * lanes)[:, half]


def order_kernel(slots, recv, arrived, out):
    lane = lax.broadcasted_iota(jnp.int32, arrived.shape[1:], 1)
    for r in range(slots):
        up = arrived[recv[r]]
        down = arrived[recv[slots + r]]
        out[r] = jnp.where(lane < HALF, down, up)


def shifted(plane, by):
    return pltpu.roll(plane, by % LANES, axis=1)


def half_weights(weights, wide, upper):
    channels, every = weights.shape[1:]
    half = every // 2
    for g in range(9):
        for r in range(3):
            w = weights[3 * g + r]
            wide[g * channels : (g + 1) * channels, r * half : (r + 1) * half] = jnp.where(
                upper, w[:, half:], w[:, :half]
            )


def conv_blocks(blocks, sets, wide, expand):
    channels = wide.shape[0] // 9
    for (row, parts), (rows, stack, prod) in zip(blocks, sets):
        size = rows.shape[0] // 4
        for at, x in parts:
            masked = x * row
            for v in range(4):
                here = pl.multiple_of(v * size + at, channels)
                rows[pl.ds(here, channels), :] = masked[:, v * LANES : (v + 1) * LANES]
    for rows, stack, prod in sets:
        size = rows.shape[0] // 4
        planes = jnp.dot(rows[...], expand[...], preferred_element_type=jnp.float32).astype(jnp.bfloat16)
        for v in range(4):
            for a in range(2):
                at = slice((2 * v + a) * LANES, (2 * v + a + 1) * LANES)
                plane = planes[v * size : (v + 1) * size, a * LANES : (a + 1) * LANES]
                stack[0:size, at] = shifted(plane, 1)
                stack[size : 2 * size, at] = plane
                stack[2 * size : 3 * size, at] = shifted(plane, -1)
    for rows, stack, prod in sets:
        prod[...] = jnp.dot(wide[...], stack[...], preferred_element_type=jnp.float32)
    for rows, stack, prod in sets:
        results = []
        for layer in range(SIDE):
            sums = []
            for q in range(3):
                total = None
                for p in range(3):
                    inside = layer + p - 1
                    if 0 <= inside < SIDE:
                        first = (3 * p + q) * channels
                        part = prod[first : first + channels, inside * LANES : (inside + 1) * LANES]
                        total = part if total is None else total + part
                sums.append(total)
            results.append(sums[1] + shifted(sums[0], PAD) + shifted(sums[2], -PAD))
        yield results


def block_parts(group, step, me, live, occ, xs):
    n = len(xs)
    channels = xs[0].shape[1]
    blocks = []
    for b in range(group):
        row = active_row(occ, step * group + b, live).astype(jnp.bfloat16)
        blocks.append((row, [(mod(me ^ key, n) * channels, x[b]) for key, x in enumerate(xs)]))
    return blocks


def near_kernel(group, me_ref, live_ref, occ, weights, expand, *refs):
    n = len(refs) - 2 - 3 * group
    xs = refs[:n]
    out, wide = refs[n : n + 2]
    channels = weights.shape[1]
    step = pl.program_id(0)
    me = me_ref[0]

    @pl.when(step == 0)
    def _():
        half_weights(weights, wide, div(me, n) == 1)

    blocks = block_parts(group, step, me, live_ref[0], occ, xs)
    sets = [refs[n + 2 + 3 * b : n + 5 + 3 * b] for b in range(group)]
    for b, results in enumerate(conv_blocks(blocks, sets, wide, expand)):
        for layer, result in enumerate(results):
            out[step * group + b, :, layer * LANES : (layer + 1) * LANES] = result


def far_kernel(group, me_ref, live_ref, occ, weights, expand, gather, near, *refs):
    n = len(refs) - 5 - 3 * group
    xs = refs[:n]
    out, rim, shell = refs[n : n + 3]
    wide, packed = refs[n + 3 : n + 5]
    channels = weights.shape[1]
    step = pl.program_id(0)
    me = me_ref[0]

    @pl.when(step == 0)
    def _():
        half_weights(weights, wide, div(me, n) == 0)

    blocks = block_parts(group, step, me, live_ref[0], occ, xs)
    sets = [refs[n + 5 + 3 * b : n + 8 + 3 * b] for b in range(group)]
    for b, results in enumerate(conv_blocks(blocks, sets, wide, expand)):
        for layer, result in enumerate(results):
            at = slice(layer * LANES, (layer + 1) * LANES)
            total = result + near[step * group + b, :, at]
            out[b, :, at] = total
            if 0 < layer < SIDE - 1:
                packed[b, :, (layer - 1) * LANES : layer * LANES] = total.astype(jnp.bfloat16)
            else:
                side = slice(LANES * (layer > 0), LANES * (layer > 0) + LANES)
                rim[step * group + b, :, side] = total
    picked = jnp.dot(
        packed[...].reshape(group * channels, (SIDE - 2) * LANES),
        gather[LANES : (SIDE - 1) * LANES, :],
        preferred_element_type=jnp.float32,
    )
    shell[pl.ds(step * group, group)] = picked.astype(jnp.bfloat16).reshape(packed.shape[:2] + shell.shape[2:])


def edge_mask(lane, quarter, e):
    return jnp.logical_and((lane >> 5) == quarter, ((lane >> 3) & 3) == e)


def halo_kernel(slots, cap, me_ref, send, weights, expand, gather, shell, base, *refs):
    n = len(refs) - 8
    hs = refs[:n]
    added, faces = refs[n : n + 2]
    wide, rows, stack, prod, packed, edges = refs[n + 2 :]
    channels, every = weights.shape[1:]
    me = me_ref[0]
    for side in range(2):
        for g in range(3):
            for r in range(3):
                wide[side, g * channels : (g + 1) * channels, r * every : (r + 1) * every] = weights[
                    18 * side + 3 * g + r
                ]
    for r in range(slots):
        for key, h in enumerate(hs):
            at = pl.multiple_of((me ^ key) * channels + r * every, channels)
            rows[pl.ds(at, channels), :] = h[r]
    for r in range(slots):
        planes = jnp.dot(
            rows[r * every : (r + 1) * every, :], expand[...], preferred_element_type=jnp.float32
        ).astype(jnp.bfloat16)
        at = slice(r * LANES, (r + 1) * LANES)
        for side in range(2):
            plane = planes[:, (1 - side) * LANES : (2 - side) * LANES]
            stack[side, 0:every, at] = shifted(plane, 1)
            stack[side, every : 2 * every, at] = plane
            stack[side, 2 * every : 3 * every, at] = shifted(plane, -1)
    for side in range(2):
        prod[side] = jnp.dot(wide[side], stack[side], preferred_element_type=jnp.float32)
    for r in range(slots):
        at = slice(r * LANES, (r + 1) * LANES)
        for side in range(2):
            sums = [prod[side, q * channels : (q + 1) * channels, at] for q in range(3)]
            result = sums[1] + shifted(sums[0], PAD) + shifted(sums[2], -PAD)
            here = slice(side * LANES, (side + 1) * LANES)
            added[r, :, here] = result
            packed[r, :, here] = (base[r, :, here] + result).astype(jnp.bfloat16)
    picked = jnp.dot(packed[...].reshape(slots * channels, 2 * LANES), gather[...], preferred_element_type=jnp.float32)
    lane = lax.broadcasted_iota(jnp.int32, (channels, LANES), 1)
    for s in range(slots):
        mine = picked[s * channels : (s + 1) * channels].astype(jnp.bfloat16) + shell[s]
        for d in range(2):
            pair = mine[:, d * LANES : (d + 1) * LANES]
            faces[send[(2 * d + 1) * slots + s], :, :HALF] = pair[:, :HALF]
            faces[send[2 * d * slots + s], :, HALF:] = pair[:, HALF:]
        edge = mine[:, 2 * LANES :].astype(jnp.float32)
        for e in range(4):
            slot = send[(4 + e) * slots + s]
            pltpu.store(edges.at[slot >> 2], edge, mask=edge_mask(lane, slot & 3, e))
    quarter = slots // 4
    for peer in range(edges.shape[0] // quarter):
        at = peer * (2 * cap + quarter) + 2 * cap
        faces[at : at + quarter] = edges[peer * quarter : (peer + 1) * quarter].astype(jnp.bfloat16)


def squeeze_kernel(part, bias, squeeze, base, added, out):
    for n in range(part):
        b = pl.program_id(0) * part + n
        for v in range(4):
            pair = base[n, :, 2 * v * LANES : 2 * (v + 1) * LANES] + bias[...]
            if v in (0, 3):
                extra = added[b, :, LANES * (v > 0) : LANES * (v > 0) + LANES]
                zero = jnp.zeros_like(extra)
                pair = pair + jnp.concatenate([extra, zero] if v == 0 else [zero, extra], axis=1)
            total = None
            for _ in range(3):
                term = pair.astype(jnp.bfloat16)
                pair = pair - term.astype(jnp.float32)
                flat = jnp.dot(term, squeeze[...], preferred_element_type=jnp.float32)
                total = flat if total is None else total + flat
            out[b, :, v * LANES : (v + 1) * LANES] = total


def finish_kernel(slots, recv, live_ref, occ, scatter, base, faces, out, shell):
    channels = base.shape[1]
    live = live_ref[0]
    lane = lax.broadcasted_iota(jnp.int32, (channels, LANES), 1)
    for r in range(slots):
        for d in range(2):
            up = faces[recv[2 * d * slots + r]]
            down = faces[recv[(2 * d + 1) * slots + r]]
            shell[r, :, d * LANES : (d + 1) * LANES] = jnp.where(lane < HALF, down, up)
        total = jnp.zeros((channels, LANES), jnp.bfloat16)
        for e in range(4):
            slot = recv[(4 + e) * slots + r]
            total = jnp.where(edge_mask(lane, slot & 3, e), faces[slot >> 2], total)
        shell[r, :, 2 * LANES :] = total
    added = jnp.dot(
        shell[...].reshape(slots * channels, 3 * LANES), scatter[...], preferred_element_type=jnp.float32
    )
    for r in range(slots):
        summed = base[r] + added[r * channels : (r + 1) * channels]
        out[r] = (summed * active_row(occ, r, live)).astype(jnp.bfloat16)


def spread(x, axis, near, size):
    have = {0: x}
    bit = near >> 1
    while bit:
        for key in list(have):
            have[key ^ bit] = lax.ppermute(have[key], axis, [(n, n ^ bit) for n in range(size)])
        bit >>= 1
    return [have[key] for key in range(near)]


def spread_direct(x, axis, size):
    return [x] + [lax.ppermute(x, axis, [(n, n ^ key) for n in range(size)]) for key in range(1, size)]


def shards(features, weights, bias, occupancy, live, neighbours):
    slots, channels, voxels = features.shape
    peers = lax.axis_size("blk")
    members = lax.axis_size("ch")
    cap = max(2, 2 * slots // peers)
    every = channels * members
    group = 8 if slots % 8 == 0 else slots
    part = 4
    bf16, f32, i32 = jnp.bfloat16, jnp.float32, jnp.int32
    smem = pl.BlockSpec(memory_space=pltpu.SMEM)
    vmem = pl.BlockSpec(memory_space=pltpu.VMEM)
    resident = lambda x: pltpu.with_memory_space_constraint(x, pltpu.VMEM)
    params = pltpu.CompilerParams(vmem_limit_bytes=VMEM_LIMIT)
    expand, gather, scatter = (jnp.asarray(t, bf16) for t in tables())
    squeeze = jnp.asarray(tables()[0].T, bf16)
    outermost = jnp.asarray(np.concatenate([tables()[1][:LANES], tables()[1][-LANES:]]), bf16)
    place = lax.axis_index("blk").astype(i32).reshape(1)
    member = lax.axis_index("ch").astype(i32).reshape(1)
    nbr = neighbours.transpose(1, 2, 0)

    def table(kinds, name, nbr):
        return pl.pallas_call(
            functools.partial(table_kernel, kinds, peers, cap, slots),
            out_shape=jax.ShapeDtypeStruct((len(kinds) * slots,), i32),
            in_specs=[smem, smem],
            out_specs=smem,
            scratch_shapes=[pltpu.SMEM((len(kinds) * peers,), i32)],
            name=name,
        )(place, nbr)

    corner = pl.BlockSpec((slots, channels, LANES), lambda n: (0, 0, 0))
    corner_last = pl.BlockSpec((slots, channels, LANES), lambda n: (0, 0, voxels // LANES - 1))
    outgoing = pl.pallas_call(
        functools.partial(pack_kernel, peers, cap, slots),
        grid=(1,),
        out_shape=jax.ShapeDtypeStruct((peers * cap, channels, LANES), bf16),
        in_specs=[smem, smem, smem, vmem, corner, corner_last],
        out_specs=vmem,
        scratch_shapes=[pltpu.SMEM((2 * peers,), i32)],
        compiler_params=params,
        name="pack_layers",
    )(place, live, nbr, occupancy, features, features)
    outgoing, shipped = lax.optimization_barrier((outgoing, features))
    half = members // 2
    across = lax.ppermute(shipped, "ch", [(n, n ^ half) for n in range(members)])
    beside = spread(shipped, "ch", half, members)
    arrived = lax.all_to_all(outgoing, "blk", split_axis=0, concat_axis=0, tiled=True)

    per_block = lambda width: pl.BlockSpec((group, channels, width), lambda n: (n, 0, 0))
    some = lambda width: pl.BlockSpec((part, channels, width), lambda n: (n, 0, 0))
    buffers = [
        pltpu.VMEM((4 * half * channels, LANES), bf16),
        pltpu.VMEM((3 * half * channels, SIDE * LANES), bf16),
        pltpu.VMEM((9 * channels, SIDE * LANES), f32),
    ] * group
    wide = pltpu.VMEM((9 * channels, 3 * half * channels), bf16)
    near = pl.pallas_call(
        functools.partial(near_kernel, group),
        grid=(slots // group,),
        out_shape=pltpu.VMEM((slots, channels, SIDE * LANES), f32),
        in_specs=[smem, smem, vmem, vmem, vmem] + [per_block(voxels)] * half,
        out_specs=vmem,
        scratch_shapes=[wide] + buffers,
        compiler_params=params,
        name="convolve_near",
    )(member, live, occupancy, weights, expand, *beside)
    near, later = lax.optimization_barrier((near, nbr))
    across, near = lax.optimization_barrier((across, near))
    remote = spread(across, "ch", half, members)

    send, incoming = pl.pallas_call(
        functools.partial(early_kernel, peers, cap, slots),
        out_shape=(jax.ShapeDtypeStruct((8 * slots,), i32), jax.ShapeDtypeStruct((2 * slots,), i32)),
        in_specs=[smem, smem],
        out_specs=(smem, smem),
        scratch_shapes=[pltpu.SMEM((8 * peers,), i32), pltpu.SMEM((2 * peers,), i32)],
        name="early_tables",
    )(place, later)
    arrived, incoming = lax.optimization_barrier((arrived, incoming))
    layers = pl.pallas_call(
        functools.partial(order_kernel, slots),
        out_shape=pltpu.VMEM((slots, channels, LANES), bf16),
        in_specs=[smem, vmem],
        out_specs=vmem,
        compiler_params=params,
        name="order_layers",
    )(incoming, resident(arrived))
    halo = spread_direct(layers, "ch", members)

    *remote, _ = lax.optimization_barrier((*remote, layers))
    base, rim, shell = pl.pallas_call(
        functools.partial(far_kernel, group),
        grid=(slots // group,),
        out_shape=(
            jax.ShapeDtypeStruct((slots, channels, SIDE * LANES), f32),
            pltpu.VMEM((slots, channels, 2 * LANES), f32),
            pltpu.VMEM((slots, channels, 3 * LANES), bf16),
        ),
        in_specs=[smem, smem, vmem, vmem, vmem, vmem, vmem] + [per_block(voxels)] * half,
        out_specs=(per_block(SIDE * LANES), vmem, vmem),
        scratch_shapes=[wide, pltpu.VMEM((group, channels, (SIDE - 2) * LANES), bf16)] + buffers,
        compiler_params=params,
        name="convolve_far",
    )(member, live, occupancy, weights, expand, gather, resident(near), *[resident(x) for x in remote])

    added, faces = pl.pallas_call(
        functools.partial(halo_kernel, slots, cap),
        out_shape=(
            pltpu.VMEM((slots, channels, 2 * LANES), f32),
            pltpu.VMEM((peers * (2 * cap + slots // 4), channels, LANES), bf16),
        ),
        in_specs=[smem, smem, vmem, vmem, vmem, vmem, vmem] + [vmem] * members,
        out_specs=(vmem, vmem),
        scratch_shapes=[
            pltpu.VMEM((2, 3 * channels, 3 * every), bf16),
            pltpu.VMEM((slots * every, LANES), bf16),
            pltpu.VMEM((2, 3 * every, slots * LANES), bf16),
            pltpu.VMEM((2, 3 * channels, slots * LANES), f32),
            pltpu.VMEM((slots, channels, 2 * LANES), bf16),
            pltpu.VMEM((peers * slots // 4, channels, LANES), f32),
        ],
        compiler_params=params,
        name="convolve_halo",
    )(
        member, send, weights, expand, outermost, resident(shell), resident(rim),
        *[resident(x) for x in halo],
    )

    faces = lax.all_to_all(faces, "blk", split_axis=0, concat_axis=0, tiled=True)

    base = pl.pallas_call(
        functools.partial(squeeze_kernel, part),
        grid=(slots // part,),
        out_shape=pltpu.VMEM((slots, channels, voxels), f32),
        in_specs=[vmem, vmem, some(SIDE * LANES), vmem],
        out_specs=vmem,
        compiler_params=params,
        name="squeeze_planes",
    )(bias[:, None], squeeze, base, resident(added))

    return pl.pallas_call(
        functools.partial(finish_kernel, slots),
        out_shape=jax.ShapeDtypeStruct((slots, channels, voxels), bf16),
        in_specs=[smem, smem] + [vmem] * 4,
        out_specs=vmem,
        scratch_shapes=[pltpu.VMEM((slots, channels, 3 * LANES), bf16)],
        compiler_params=params,
        name="finish",
    )(
        table(tuple(range(8)), "slot_table", nbr), live, occupancy, scatter, resident(base),
        resident(faces),
    )


def solution(mesh):
    in_specs = (P("blk", "ch", None), P(None, "ch", None), P("ch"), P("blk", None), P("blk"), P())
    out_specs = P("blk", "ch", None)
    return jax.shard_map(shards, mesh=mesh, in_specs=in_specs, out_specs=out_specs, check_vma=False)
```

time: 83.2 us -> 64.8 us (0.78)
  waiting for transfers between devices: 29.4 us -> 13.3 us
  local copies, waits for them, and re-layouts: 4.74 us -> 1.48 us
  starting transfers between devices: 14.7 us -> 16.9 us
  Pallas kernels: 33.1 us -> 31.8 us
    ppermute x6 -> x2, waiting for transfers between devices: 8.06 us -> 0.01 us  [spread(): lax.ppermute(have[key], axis, [(n, n ^ bit) for n in range(size)])]
    all_to_all x1, waiting for transfers between devices: 19.8 us -> 12.6 us  [shards(): lax.all_to_all(faces, 'blk', split_axis=0, concat_axis=0, tiled=True)]
    ppermute x0 -> x4, starting transfers between devices: none -> 4.82 us  [the longest x1 2.51 us: shards(): lax.ppermute(shipped, 'ch', [(n, n ^ half) for n in range(members)])]
    ppermute x6 -> x2, starting transfers between devices: 3.58 us -> 0.5 us  [spread(): lax.ppermute(have[key], axis, [(n, n ^ bit) for n in range(size)])]
    unnamed x21 -> x4, local copies, waits for them, and re-layouts: 3.28 us -> 0.79 us
    all_to_all x1, waiting for transfers between devices: 1.58 us -> 0.01 us  [shards(): lax.all_to_all(outgoing, 'blk', split_axis=0, concat_axis=0, tiled=True)]
    pallas_call x4 -> x8, Pallas kernels: 31.2 us -> 29.8 us  [the longest x1 7.18 us: shards(): pl.pallas_call(functools.partial(far_kernel, group), grid=(slots // group...]
  transfers between devices with their start and end apart: 8 -> 8, of which waited for: 5 -> 2; matrix products, arithmetic and copies ran while one was open for 3% -> 1% of each run, Pallas kernels for 10% -> 37%
where the time goes in v1:
time: 64.8 us; the launch traced here: 64.3 us
  Pallas kernels  31.8 us (49%)
  starting transfers between devices  16.9 us (26%)
  waiting for transfers between devices  13.3 us (21%)
  local copies, waits for them, and re-layouts  1.48 us (2%)
  between operations  0.74 us (1%)
    all_to_all x1, waiting for transfers between devices, shards(): lax.all_to_all(faces, 'blk', split_axis=0, concat_axis=0, tiled=True)  12.6 us
    pallas_call x1, Pallas kernels, shards(): pl.pallas_call(functools.partial(far_kernel, group), grid=(slots // group...  7.18 us
    all_to_all x1, starting transfers between devices, shards(): lax.all_to_all(faces, 'blk', split_axis=0, concat_axis=0, tiled=True)  5.81 us
    all_to_all x1, starting transfers between devices, shards(): lax.all_to_all(outgoing, 'blk', split_axis=0, concat_axis=0, tiled=True)  5.81 us
    pallas_call x1, Pallas kernels, shards(): pl.pallas_call(functools.partial(near_kernel, group), grid=(slots // grou...  5.53 us
    pallas_call x1, Pallas kernels, shards(): pl.pallas_call(functools.partial(squeeze_kernel, part), grid=(slots // pa...  3.97 us
    pallas_call x1, Pallas kernels, table(): pl.pallas_call(functools.partial(table_kernel, kinds, peers, cap, slots),...  3.58 us
    pallas_call x1, Pallas kernels, shards(): pl.pallas_call(functools.partial(halo_kernel, slots, cap), out_shape=(plt...  3.5 us
  transfers between devices with their start and end apart: 8, of which 2 were waited for; matrix products, arithmetic and copies ran while one was open for 1% of the time, Pallas kernels for 37%

profile of v1, /device:TPU:0, one launch (start us, length us, event | category | flops | bytes accessed | tf_op | source)
XLA Modules:
  0.0 64.3 jit_solution(7830609069475565120)
XLA Ops:
  0.7 2.0 %pack_layers.1 = bf16[32,32,128]{2,1,0:T(8,128)(2,1)} custom-call(s32[1]{0:T(128)} %bitcast.me_ref, s32[1]{0:T(128)S(6)} %copy.13.live_ref, s32[3,2,128]{2,1,0:T(2,128)} %bitcast.4, s32[16,512]{1,0:T(8,128)} %occ.7, bf16[16,32,512]{2,1,0:T(8,128)(2,1)} %refs_0_, bf16[16,32,512]{2,1,0:T(8,128)(2,1)} %refs_0_), custom_call_target="tpu_custom_call" | custom-call | tf_op jit(solution)/shard_map/pack_layers/pallas_call | solution.py:442
  2.6 0.5 collective-permute-start.1
  3.1 2.5 %collective-permute-start = (bf16[16,32,512]{2,1,0:T(8,128)(2,1)}, bf16[16,32,512]{2,1,0:T(8,128)(2,1)S(1)}, u32[]{:S(2)}, u32[]{:S(2)}) collective-permute-start(bf16[16,32,512]{2,1,0:T(8,128)(2,1)} %refs_0_), channel_id=1, source_target_pairs={{0,2},{1,3},{2,0},{3,1},{4,6},{5,7},{6,4},{7,5},{8,10},{9,11},{10,... | collective-permute-start | bytes 1572872 | tf_op jit(solution)/shard_map/ppermute | solution.py:454
  5.6 5.8 %all-to-all-start = ((bf16[32,32,128]{2,1,0:T(8,128)(2,1)}), bf16[32,32,128]{2,1,0:T(8,128)(2,1)S(1)}, u32[]{:S(2)}, u32[]{:S(2)}) async-start(bf16[32,32,128]{2,1,0:T(8,128)(2,1)} %pack_layers.1), calls=%async_computation | async-start | bytes 524288 | tf_op jit(solution)/shard_map/all_to_all | solution.py:456
  11.4 0.0 collective-permute-done.1.refs_1_
  11.4 0.0 copy-start
  11.5 0.8 %copy-done = bf16[16,32,512]{2,1,0:T(8,128)(2,1)} copy-done((bf16[16,32,512]{2,1,0:T(8,128)(2,1)}, bf16[16,32,512]{2,1,0:T(8,128)(2,1)S(1)}, u32[]{:S(2)}) %copy-start) | copy-done | bytes 524312
  12.2 5.5 %convolve_near.1.near = f32[16,32,1024]{2,1,0:T(8,128)S(1)} custom-call(s32[1]{0:T(128)} %bitcast.3.me_ref, s32[1]{0:T(128)S(6)} %copy.13.live_ref, s32[16,512]{1,0:T(8,128)} %occ.7, bf16[27,32,128]{2,1,0:T(8,128)(2,1)} %weights.5, bf16[128,256]{1,0:T(8,128)(2,1)} %constant.19.clone.expand, bf16[16,32,512]{2,1,0:T(8,128)(2,1)} %refs_0_, ...), custom_call_target="tpu_custom_call" | custom-call | tf_op jit(solution)/shard_map/convolve_near/pallas_call | solution.py:466
  17.8 0.7 %collective-permute-done.refs_0_ = bf16[16,32,512]{2,1,0:T(8,128)(2,1)S(1)} collective-permute-done((bf16[16,32,512]{2,1,0:T(8,128)(2,1)}, bf16[16,32,512]{2,1,0:T(8,128)(2,1)S(1)}, u32[]{:S(2)}, u32[]{:S(2)}) %collective-permute-start) | collective-permute-done | bytes 524320 | tf_op jit(solution)/shard_map/ppermute | solution.py:454
  18.4 0.0 collective-permute-start.2
  18.4 3.1 %early_tables.1 = (s32[128]{0:T(128)}, s32[32]{0:T(128)}) custom-call(s32[1]{0:T(128)} %bitcast.me_ref, s32[3,2,128]{2,1,0:T(2,128)} %bitcast.5), custom_call_target="tpu_custom_call" | custom-call | tf_op jit(solution)/shard_map/early_tables/pallas_call | solution.py:480
  21.5 0.0 all-to-all-done.arrived
  21.5 0.7 %order_layers.1.refs_0_ = bf16[16,32,128]{2,1,0:T(8,128)(2,1)S(1)} custom-call(s32[32]{0:T(128)} %get-tuple-element.29.recv, bf16[32,32,128]{2,1,0:T(8,128)(2,1)S(1)} %all-to-all-done.arrived), custom_call_target="tpu_custom_call" | custom-call | tf_op jit(solution)/shard_map/order_layers/pallas_call | solution.py:489
  22.3 0.6 collective-permute-start.3
  22.8 1.7 %collective-permute-start.4 = (bf16[16,32,128]{2,1,0:T(8,128)(2,1)S(1)}, bf16[16,32,128]{2,1,0:T(8,128)(2,1)S(1)}, u32[]{:S(2)}, u32[]{:S(2)}) collective-permute-start(bf16[16,32,128]{2,1,0:T(8,128)(2,1)S(1)} %order_layers.1.refs_0_), channel_id=1, source_target_pairs={{0,2},{1,3},{2,0},{3,1},{4,6},{5,7},{6,4},{7,5},{8,10},{9,11},{10,... | collective-permute-start | bytes 393224 | tf_op jit(solution)/shard_map/ppermute | solution.py:407
  24.6 0.0 collective-permute-start.5
  24.6 0.0 collective-permute-done.2.refs_1_
  24.6 7.2 %convolve_far.1 = (f32[16,32,1024]{2,1,0:T(8,128)}, f32[16,32,256]{2,1,0:T(8,128)S(1)}, bf16[16,32,384]{2,1,0:T(8,128)(2,1)S(1)}) custom-call(s32[1]{0:T(128)} %bitcast.3.me_ref, s32[1]{0:T(128)S(6)} %copy.13.live_ref, s32[16,512]{1,0:T(8,128)} %occ.7, bf16[27,32,128]{2,1,0:T(8,128)(2,1)} %weights.5, bf16[128,256]{1,0:T(8,128)(2,1)} %constant.19.clone.expand, ...), custom_call_target="tpu_custom_call" | custom-call | tf_op jit(solution)/shard_map/convolve_far/pallas_call | solution.py:500
  31.8 0.0 copy-start.1
  31.8 0.0 collective-permute-done.3.refs_1_
  31.8 0.0 collective-permute-done.4.refs_2_
  31.8 0.0 collective-permute-done.5.refs_3_
  31.8 3.5 %convolve_halo.1 = (f32[16,32,256]{2,1,0:T(8,128)S(1)}, bf16[96,32,128]{2,1,0:T(8,128)(2,1)}) custom-call(s32[1]{0:T(128)} %bitcast.3.me_ref, s32[128]{0:T(128)} %get-tuple-element.34.send, bf16[27,32,128]{2,1,0:T(8,128)(2,1)} %weights.5, bf16[128,256]{1,0:T(8,128)(2,1)} %constant.19.clone.expand, bf16[256,384]{1,0:T(8,128)(2,1)} %constant.23.clone.gather, ...), custom_call_target="tpu_custom_call" | custom-call | tf_op jit(solution)/shard_map/convolve_halo/pallas_call | solution.py:515
  35.3 5.8 %all-to-all-start.1 = ((bf16[96,32,128]{2,1,0:T(8,128)(2,1)}), bf16[96,32,128]{2,1,0:T(8,128)(2,1)S(1)}, u32[]{:S(2)}, u32[]{:S(2)}) async-start(bf16[96,32,128]{2,1,0:T(8,128)(2,1)} %get-tuple-element.38), calls=%async_computation.1 | async-start | bytes 1572864 | tf_op jit(solution)/shard_map/all_to_all | solution.py:538
  41.1 3.6 %slot_table.1.recv = s32[128]{0:T(128)} custom-call(s32[1]{0:T(128)} %bitcast.me_ref, s32[3,2,128]{2,1,0:T(2,128)} %bitcast.6), custom_call_target="tpu_custom_call" | custom-call | tf_op jit(solution)/shard_map/slot_table/pallas_call | solution.py:431
  44.7 0.0 copy-done.1
  44.7 0.7 %copy.12.bias = f32[32,1]{1,0:T(8,128)} copy(f32[32,1]{0,1:T(1,128)S(1)} %bitcast.7) | data formatting | bytes 256 | tf_op jit(solution)/shard_map/broadcast_in_dim | solution.py:548
  45.4 4.0 %squeeze_planes.1.base = f32[16,32,512]{2,1,0:T(8,128)S(1)} custom-call(f32[32,1]{1,0:T(8,128)} %copy.12.bias, bf16[256,128]{1,0:T(8,128)(2,1)} %constant.22.clone.squeeze, f32[16,32,1024]{2,1,0:T(8,128)} %get-tuple-element.33.base, f32[16,32,256]{2,1,0:T(8,128)S(1)} %get-tuple-element.37.added), custom_call_target="tpu_custom_call" | custom-call | tf_op jit(solution)/shard_map/squeeze_planes/pallas_call | solution.py:540
  49.4 12.6 %all-to-all-done.1.faces = bf16[96,32,128]{2,1,0:T(8,128)(2,1)S(1)} async-done(((bf16[96,32,128]{2,1,0:T(8,128)(2,1)}), bf16[96,32,128]{2,1,0:T(8,128)(2,1)S(1)}, u32[]{:S(2)}, u32[]{:S(2)}) %all-to-all-start.1) | async-done | bytes 786464 | tf_op jit(solution)/shard_map/all_to_all | solution.py:538
  62.0 2.3 %finish.1 = bf16[16,32,512]{2,1,0:T(8,128)(2,1)} custom-call(s32[128]{0:T(128)} %slot_table.1.recv, s32[1]{0:T(128)S(6)} %copy.13.live_ref, s32[16,512]{1,0:T(8,128)} %occ.7, bf16[384,512]{1,0:T(8,128)(2,1)} %constant.21.clone.scatter, f32[16,32,512]{2,1,0:T(8,128)S(1)} %squeeze_planes.1.base, bf16[96,32,128]{2,1,0:T(8,128)(2,1)S(1)} %all-to-all-done.1.faces), custom_call_target="tpu_custom_call" | custom-call | tf_op jit(solution)/shard_map/finish/pallas_call | solution.py:550
Async XLA Ops:
  2.6 8.8 %collective-permute-start.1 = (bf16[16,32,512]{2,1,0:T(8,128)(2,1)}, bf16[16,32,512]{2,1,0:T(8,128)(2,1)S(1)}, u32[]{:S(2)}, u32[]{:S(2)}) collective-permute-start(bf16[16,32,512]{2,1,0:T(8,128)(2,1)} %refs_0_), channel_id=1, source_target_pairs={{0,1},{1,0},{2,3},{3,2},{4,5},{5,4},{6,7},{7,6},{8,9},{9,8},{10,11... | collective-permute-start | bytes 1572872 | tf_op jit(solution)/shard_map/ppermute | solution.py:401
  3.1 15.3 %collective-permute-start = (bf16[16,32,512]{2,1,0:T(8,128)(2,1)}, bf16[16,32,512]{2,1,0:T(8,128)(2,1)S(1)}, u32[]{:S(2)}, u32[]{:S(2)}) collective-permute-start(bf16[16,32,512]{2,1,0:T(8,128)(2,1)} %refs_0_), channel_id=1, source_target_pairs={{0,2},{1,3},{2,0},{3,1},{4,6},{5,7},{6,4},{7,5},{8,10},{9,11},{10,... | collective-permute-start | bytes 1572872 | tf_op jit(solution)/shard_map/ppermute | solution.py:454
  5.6 15.9 %all-to-all-start = ((bf16[32,32,128]{2,1,0:T(8,128)(2,1)}), bf16[32,32,128]{2,1,0:T(8,128)(2,1)S(1)}, u32[]{:S(2)}, u32[]{:S(2)}) async-start(bf16[32,32,128]{2,1,0:T(8,128)(2,1)} %pack_layers.1), calls=%async_computation | async-start | bytes 524288 | tf_op jit(solution)/shard_map/all_to_all | solution.py:456
  11.4 0.8 %copy-start = (bf16[16,32,512]{2,1,0:T(8,128)(2,1)}, bf16[16,32,512]{2,1,0:T(8,128)(2,1)S(1)}, u32[]{:S(2)}) copy-start(bf16[16,32,512]{2,1,0:T(8,128)(2,1)S(1)} %collective-permute-done.1.refs_1_) | copy-start | bytes 1572868
  18.4 6.1 %collective-permute-start.2 = (bf16[16,32,512]{2,1,0:T(8,128)(2,1)S(1)}, bf16[16,32,512]{2,1,0:T(8,128)(2,1)S(1)}, u32[]{:S(2)}, u32[]{:S(2)}) collective-permute-start(bf16[16,32,512]{2,1,0:T(8,128)(2,1)S(1)} %collective-permute-done.refs_0_), channel_id=1, source_target_pairs={{0,1},{1,0},{2,3},{3,2},{4,5},{5,4},{6,7},{7,6},{8,9},{9,8},{10,11... | collective-permute-start | bytes 1572872 | tf_op jit(solution)/shard_map/ppermute | solution.py:401
  22.3 9.5 %collective-permute-start.3 = (bf16[16,32,128]{2,1,0:T(8,128)(2,1)S(1)}, bf16[16,32,128]{2,1,0:T(8,128)(2,1)S(1)}, u32[]{:S(2)}, u32[]{:S(2)}) collective-permute-start(bf16[16,32,128]{2,1,0:T(8,128)(2,1)S(1)} %order_layers.1.refs_0_), channel_id=1, source_target_pairs={{0,1},{1,0},{2,3},{3,2},{4,5},{5,4},{6,7},{7,6},{8,9},{9,8},{10,11... | collective-permute-start | bytes 393224 | tf_op jit(solution)/shard_map/ppermute | solution.py:407
  22.8 8.9 %collective-permute-start.4 = (bf16[16,32,128]{2,1,0:T(8,128)(2,1)S(1)}, bf16[16,32,128]{2,1,0:T(8,128)(2,1)S(1)}, u32[]{:S(2)}, u32[]{:S(2)}) collective-permute-start(bf16[16,32,128]{2,1,0:T(8,128)(2,1)S(1)} %order_layers.1.refs_0_), channel_id=1, source_target_pairs={{0,2},{1,3},{2,0},{3,1},{4,6},{5,7},{6,4},{7,5},{8,10},{9,11},{10,... | collective-permute-start | bytes 393224 | tf_op jit(solution)/shard_map/ppermute | solution.py:407
  24.6 7.2 %collective-permute-start.5 = (bf16[16,32,128]{2,1,0:T(8,128)(2,1)S(1)}, bf16[16,32,128]{2,1,0:T(8,128)(2,1)S(1)}, u32[]{:S(2)}, u32[]{:S(2)}) collective-permute-start(bf16[16,32,128]{2,1,0:T(8,128)(2,1)S(1)} %order_layers.1.refs_0_), channel_id=1, source_target_pairs={{0,3},{1,2},{2,1},{3,0},{4,7},{5,6},{6,5},{7,4},{8,11},{9,10},{10,... | collective-permute-start | bytes 393224 | tf_op jit(solution)/shard_map/ppermute | solution.py:407
  31.8 12.9 %copy-start.1 = (f32[32]{0:T(128)S(1)}, f32[32]{0:T(128)}, u32[]{:S(2)}) copy-start(f32[32]{0:T(128)} %param.13) | copy-start | bytes 388
  35.3 26.7 %all-to-all-start.1 = ((bf16[96,32,128]{2,1,0:T(8,128)(2,1)}), bf16[96,32,128]{2,1,0:T(8,128)(2,1)S(1)}, u32[]{:S(2)}, u32[]{:S(2)}) async-start(bf16[96,32,128]{2,1,0:T(8,128)(2,1)} %get-tuple-element.38), calls=%async_computation.1 | async-start | bytes 1572864 | tf_op jit(solution)/shard_map/all_to_all | solution.py:538

commit v2 on v1

--- a/solution.py
+++ b/solution.py
@@ -69,20 +69,25 @@
     return (x + (x >> 16)) & 0x3F
 
 
-def clear(ref, size):
+def each(size, step, unrolled):
+    if unrolled:
+        for n in range(size):
+            step(n, 0)
+    else:
+        lax.fori_loop(0, size, step, 0)
+
+
+def clear(ref, size, unrolled=False):
     def step(n, _):
         ref[n] = 0
         return 0
 
-    lax.fori_loop(0, size, step, 0)
+    each(size, step, unrolled)
 
 
 def slot_of(kind, peer, place, cap, slots):
-    rows = 2 * cap + slots // 4
     if kind < 4:
-        return peer * rows + (FACES[kind][0] - 1) * cap + place
-    if kind < 8:
-        return (peer * rows + 2 * cap) * 4 + place
+        return peer * (2 * cap + slots // 4) + (FACES[kind][0] - 1) * cap + place
     return peer * cap + place
 
 
@@ -91,10 +96,7 @@
 
 
 def dest(nbr, b, kind):
-    if kind < 4:
-        return neighbour(nbr, b, *FACES[kind])
-    qj, qk = EDGES[kind - 4]
-    return neighbour(nbr, neighbour(nbr, b, 1, qj), 2, qk)
+    return neighbour(nbr, b, *FACES[kind])
 
 
 def source(nbr, r, kind):
@@ -107,24 +109,24 @@
     return neighbour(nbr, neighbour(nbr, r, 2, 1 - qk), 1, 1 - qj)
 
 
-def send_kernel(peers, cap, slots, me_ref, nbr, send, count):
+def send_slots(peers, cap, slots, me_ref, nbr, send, count, unrolled):
     first = me_ref[0] * slots
-    clear(count, 8 * peers)
+    clear(count, 4 * peers, unrolled)
 
     def place_of(s, _):
-        for kind in range(8):
+        for kind in range(4):
             peer = div(dest(nbr, first + s, kind), slots)
             place = count[kind * peers + peer]
             count[kind * peers + peer] = place + 1
-            send[kind * slots + s] = slot_of(kind, peer, place, cap, slots) if kind < 4 else peer * slots + place
+            send[kind * slots + s] = slot_of(kind, peer, place, cap, slots)
         return 0
 
-    lax.fori_loop(0, slots, place_of, 0)
-
-
-def table_kernel(kinds, peers, cap, slots, me_ref, nbr, recv, mask):
+    each(slots, place_of, unrolled)
+
+
+def arrival_slots(kinds, peers, cap, slots, me_ref, nbr, recv, mask, unrolled=False):
     first = me_ref[0] * slots
-    clear(mask, len(kinds) * peers)
+    clear(mask, len(kinds) * peers, unrolled)
 
     def gather(s, _):
         for n, kind in enumerate(kinds):
@@ -133,7 +135,7 @@
             mask[at] = mask[at] | (1 << mod(b, slots))
         return 0
 
-    lax.fori_loop(0, slots, gather, 0)
+    each(slots, gather, unrolled)
 
     def rank(r, _):
         for n, kind in enumerate(kinds):
@@ -143,12 +145,21 @@
             recv[n * slots + r] = slot_of(kind, peer, before, cap, slots)
         return 0
 
-    lax.fori_loop(0, slots, rank, 0)
-
-
-def early_kernel(peers, cap, slots, me_ref, nbr, send, recv, count, mask):
-    send_kernel(peers, cap, slots, me_ref, nbr, send, count)
-    table_kernel((8, 9), peers, cap, slots, me_ref, nbr, recv, mask)
+    each(slots, rank, unrolled)
+
+
+def late_kernel(peers, cap, slots, me_ref, nbr, recv, mask):
+    arrival_slots(range(4), peers, cap, slots, me_ref, nbr, recv, mask)
+    me = me_ref[0]
+
+    def place_of(r, _):
+        for kind in range(4, 8):
+            b = source(nbr, me * slots + r, kind)
+            row = div(b, slots) * (2 * cap + slots // 4) + 2 * cap
+            recv[kind * slots + r] = row * 4 + mod(b, slots)
+        return 0
+
+    lax.fori_loop(0, slots, place_of, 0)
 
 
 def active_row(occ_ref, s, live):
@@ -242,23 +253,19 @@
     return blocks
 
 
-def near_kernel(group, me_ref, live_ref, occ, weights, expand, *refs):
-    n = len(refs) - 2 - 3 * group
+def near_kernel(peers, cap, group, place_ref, me_ref, live_ref, nbr, occ, weights, expand, *refs):
+    n = len(refs) - 6 - 3 * group
     xs = refs[:n]
-    out, wide = refs[n : n + 2]
-    channels = weights.shape[1]
-    step = pl.program_id(0)
+    out, send, recv, wide, count, mask = refs[n : n + 6]
+    sets = [refs[n + 6 + 3 * b : n + 9 + 3 * b] for b in range(group)]
     me = me_ref[0]
-
-    @pl.when(step == 0)
-    def _():
-        half_weights(weights, wide, div(me, n) == 1)
-
-    blocks = block_parts(group, step, me, live_ref[0], occ, xs)
-    sets = [refs[n + 2 + 3 * b : n + 5 + 3 * b] for b in range(group)]
+    send_slots(peers, cap, group, place_ref, nbr, send, count, True)
+    arrival_slots((8, 9), peers, cap, group, place_ref, nbr, recv, mask, True)
+    half_weights(weights, wide, div(me, n) == 1)
+    blocks = block_parts(group, 0, me, live_ref[0], occ, xs)
     for b, results in enumerate(conv_blocks(blocks, sets, wide, expand)):
         for layer, result in enumerate(results):
-            out[step * group + b, :, layer * LANES : (layer + 1) * LANES] = result
+            out[b, :, layer * LANES : (layer + 1) * LANES] = result
 
 
 def far_kernel(group, me_ref, live_ref, occ, weights, expand, gather, near, *refs):
@@ -336,21 +343,17 @@
             added[r, :, here] = result
             packed[r, :, here] = (base[r, :, here] + result).astype(jnp.bfloat16)
     picked = jnp.dot(packed[...].reshape(slots * channels, 2 * LANES), gather[...], preferred_element_type=jnp.float32)
-    lane = lax.broadcasted_iota(jnp.int32, (channels, LANES), 1)
     for s in range(slots):
         mine = picked[s * channels : (s + 1) * channels].astype(jnp.bfloat16) + shell[s]
         for d in range(2):
             pair = mine[:, d * LANES : (d + 1) * LANES]
             faces[send[(2 * d + 1) * slots + s], :, :HALF] = pair[:, :HALF]
             faces[send[2 * d * slots + s], :, HALF:] = pair[:, HALF:]
-        edge = mine[:, 2 * LANES :].astype(jnp.float32)
-        for e in range(4):
-            slot = send[(4 + e) * slots + s]
-            pltpu.store(edges.at[slot >> 2], edge, mask=edge_mask(lane, slot & 3, e))
-    quarter = slots // 4
-    for peer in range(edges.shape[0] // quarter):
-        at = peer * (2 * cap + quarter) + 2 * cap
-        faces[at : at + quarter] = edges[peer * quarter : (peer + 1) * quarter].astype(jnp.bfloat16)
+        quarter = slice((s & 3) * 4 * SIDE, ((s & 3) + 1) * 4 * SIDE)
+        edges[s >> 2, :, quarter] = mine[:, 2 * LANES :][:, quarter]
+    size = 2 * cap + slots // 4
+    for peer in range(faces.shape[0] // size):
+        faces[peer * size + 2 * cap : (peer + 1) * size] = edges[...]
 
 
 def squeeze_kernel(part, bias, squeeze, base, added, out):
@@ -427,16 +430,6 @@
     member = lax.axis_index("ch").astype(i32).reshape(1)
     nbr = neighbours.transpose(1, 2, 0)
 
-    def table(kinds, name, nbr):
-        return pl.pallas_call(
-            functools.partial(table_kernel, kinds, peers, cap, slots),
-            out_shape=jax.ShapeDtypeStruct((len(kinds) * slots,), i32),
-            in_specs=[smem, smem],
-            out_specs=smem,
-            scratch_shapes=[pltpu.SMEM((len(kinds) * peers,), i32)],
-            name=name,
-        )(place, nbr)
-
     corner = pl.BlockSpec((slots, channels, LANES), lambda n: (0, 0, 0))
     corner_last = pl.BlockSpec((slots, channels, LANES), lambda n: (0, 0, voxels // LANES - 1))
     outgoing = pl.pallas_call(
@@ -452,39 +445,33 @@
     outgoing, shipped = lax.optimization_barrier((outgoing, features))
     half = members // 2
     across = lax.ppermute(shipped, "ch", [(n, n ^ half) for n in range(members)])
+    arrived = lax.all_to_all(outgoing, "blk", split_axis=0, concat_axis=0, tiled=True)
     beside = spread(shipped, "ch", half, members)
-    arrived = lax.all_to_all(outgoing, "blk", split_axis=0, concat_axis=0, tiled=True)
 
     per_block = lambda width: pl.BlockSpec((group, channels, width), lambda n: (n, 0, 0))
     some = lambda width: pl.BlockSpec((part, channels, width), lambda n: (n, 0, 0))
-    buffers = [
+    buffers = lambda count: [
         pltpu.VMEM((4 * half * channels, LANES), bf16),
         pltpu.VMEM((3 * half * channels, SIDE * LANES), bf16),
         pltpu.VMEM((9 * channels, SIDE * LANES), f32),
-    ] * group
+    ] * count
     wide = pltpu.VMEM((9 * channels, 3 * half * channels), bf16)
-    near = pl.pallas_call(
-        functools.partial(near_kernel, group),
-        grid=(slots // group,),
-        out_shape=pltpu.VMEM((slots, channels, SIDE * LANES), f32),
-        in_specs=[smem, smem, vmem, vmem, vmem] + [per_block(voxels)] * half,
-        out_specs=vmem,
-        scratch_shapes=[wide] + buffers,
+    near, send, incoming = pl.pallas_call(
+        functools.partial(near_kernel, peers, cap, slots),
+        out_shape=(
+            pltpu.VMEM((slots, channels, SIDE * LANES), f32),
+            jax.ShapeDtypeStruct((4 * slots,), i32),
+            jax.ShapeDtypeStruct((2 * slots,), i32),
+        ),
+        in_specs=[smem, smem, smem, smem, vmem, vmem, vmem] + [vmem] * half,
+        out_specs=(vmem, smem, smem),
+        scratch_shapes=[wide, pltpu.SMEM((4 * peers,), i32), pltpu.SMEM((2 * peers,), i32)] + buffers(slots),
         compiler_params=params,
         name="convolve_near",
-    )(member, live, occupancy, weights, expand, *beside)
-    near, later = lax.optimization_barrier((near, nbr))
+    )(place, member, live, nbr, occupancy, weights, expand, *beside)
     across, near = lax.optimization_barrier((across, near))
     remote = spread(across, "ch", half, members)
 
-    send, incoming = pl.pallas_call(
-        functools.partial(early_kernel, peers, cap, slots),
-        out_shape=(jax.ShapeDtypeStruct((8 * slots,), i32), jax.ShapeDtypeStruct((2 * slots,), i32)),
-        in_specs=[smem, smem],
-        out_specs=(smem, smem),
-        scratch_shapes=[pltpu.SMEM((8 * peers,), i32), pltpu.SMEM((2 * peers,), i32)],
-        name="early_tables",
-    )(place, later)
     arrived, incoming = lax.optimization_barrier((arrived, incoming))
     layers = pl.pallas_call(
         functools.partial(order_kernel, slots),
@@ -507,7 +494,7 @@
         ),
         in_specs=[smem, smem, vmem, vmem, vmem, vmem, vmem] + [per_block(voxels)] * half,
         out_specs=(per_block(SIDE * LANES), vmem, vmem),
-        scratch_shapes=[wide, pltpu.VMEM((group, channels, (SIDE - 2) * LANES), bf16)] + buffers,
+        scratch_shapes=[wide, pltpu.VMEM((group, channels, (SIDE - 2) * LANES), bf16)] + buffers(group),
         compiler_params=params,
         name="convolve_far",
     )(member, live, occupancy, weights, expand, gather, resident(near), *[resident(x) for x in remote])
@@ -526,7 +513,7 @@
             pltpu.VMEM((2, 3 * every, slots * LANES), bf16),
             pltpu.VMEM((2, 3 * channels, slots * LANES), f32),
             pltpu.VMEM((slots, channels, 2 * LANES), bf16),
-            pltpu.VMEM((peers * slots // 4, channels, LANES), f32),
+            pltpu.VMEM((slots // 4, channels, LANES), bf16),
         ],
         compiler_params=params,
         name="convolve_halo",
@@ -547,6 +534,14 @@
         name="squeeze_planes",
     )(bias[:, None], squeeze, base, resident(added))
 
+    recv = pl.pallas_call(
+        functools.partial(late_kernel, peers, cap, slots),
+        out_shape=jax.ShapeDtypeStruct((8 * slots,), i32),
+        in_specs=[smem, smem],
+        out_specs=smem,
+        scratch_shapes=[pltpu.SMEM((4 * peers,), i32)],
+        name="late_tables",
+    )(place, nbr)
     return pl.pallas_call(
         functools.partial(finish_kernel, slots),
         out_shape=jax.ShapeDtypeStruct((slots, channels, voxels), bf16),
@@ -556,8 +551,7 @@
         compiler_params=params,
         name="finish",
     )(
-        table(tuple(range(8)), "slot_table", nbr), live, occupancy, scatter, resident(base),
-        resident(faces),
+        recv, live, occupancy, scatter, resident(base), resident(faces),
     )
 
 

time: 64.8 us -> 61.7 us (0.952)
  Pallas kernels: 31.8 us -> 28.3 us
  waiting for transfers between devices: 13.3 us -> 16 us
  starting transfers between devices: 16.9 us -> 14.7 us
    pallas_call x3 -> x2, Pallas kernels: 12.2 us -> 8.74 us  [the longest x1 5.99 us: shards(): pl.pallas_call(functools.partial(near_kernel, peers, cap, slots), out_sha...]
    all_to_all x1, waiting for transfers between devices: 0.01 us -> 2.31 us  [shards(): lax.all_to_all(outgoing, 'blk', split_axis=0, concat_axis=0, tiled=True)]
    all_to_all x1, starting transfers between devices: 5.81 us -> 3.93 us  [shards(): lax.all_to_all(faces, 'blk', split_axis=0, concat_axis=0, tiled=True)]
    all_to_all x1, waiting for transfers between devices: 12.6 us -> 13.5 us  [shards(): lax.all_to_all(faces, 'blk', split_axis=0, concat_axis=0, tiled=True)]
  transfers between devices with their start and end apart: 8 -> 8, of which waited for: 2 -> 3; matrix products, arithmetic and copies ran while one was open for 1% -> 1% of each run, Pallas kernels for 37% -> 34%
where the time goes in v2:
time: 61.7 us; the launch traced here: 61.2 us
  Pallas kernels  28.3 us (46%)
  waiting for transfers between devices  16 us (26%)
  starting transfers between devices  14.7 us (24%)
  local copies, waits for them, and re-layouts  1.48 us (2%)
  between operations  0.73 us (1%)
    all_to_all x1, waiting for transfers between devices, shards(): lax.all_to_all(faces, 'blk', split_axis=0, concat_axis=0, tiled=True)  13.5 us
    pallas_call x1, Pallas kernels, shards(): pl.pallas_call(functools.partial(far_kernel, group), grid=(slots // group...  7.15 us
    pallas_call x1, Pallas kernels, shards(): pl.pallas_call(functools.partial(near_kernel, peers, cap, slots), out_sha...  5.99 us
    all_to_all x1, starting transfers between devices, shards(): lax.all_to_all(outgoing, 'blk', split_axis=0, concat_axis=0, tiled=True)  5.81 us
    pallas_call x1, Pallas kernels, shards(): pl.pallas_call(functools.partial(squeeze_kernel, part), grid=(slots // pa...  3.97 us
    all_to_all x1, starting transfers between devices, shards(): lax.all_to_all(faces, 'blk', split_axis=0, concat_axis=0, tiled=True)  3.93 us
    pallas_call x1, Pallas kernels, shards(): pl.pallas_call(functools.partial(halo_kernel, slots, cap), out_shape=(plt...  3.51 us
    pallas_call x1, Pallas kernels, shards(): pl.pallas_call(functools.partial(late_kernel, peers, cap, slots), out_sha...  2.75 us
  transfers between devices with their start and end apart: 8, of which 3 were waited for; matrix products, arithmetic and copies ran while one was open for 1% of the time, Pallas kernels for 34%

profile of v2, /device:TPU:0, one launch (start us, length us, event | category | flops | bytes accessed | tf_op | source)
XLA Modules:
  0.0 61.2 jit_solution(4508692571303936876)
XLA Ops:
  0.7 2.0 %pack_layers.1 = bf16[32,32,128]{2,1,0:T(8,128)(2,1)} custom-call(s32[1]{0:T(128)} %bitcast.me_ref.place_ref, s32[1]{0:T(128)S(6)} %copy.13.live_ref, s32[3,2,128]{2,1,0:T(2,128)} %bitcast.4, s32[16,512]{1,0:T(8,128)} %occ.7, bf16[16,32,512]{2,1,0:T(8,128)(2,1)} %refs_0_, bf16[16,32,512]{2,1,0:T(8,128)(2,1)} %refs_0_), custom_call_target="tpu_custom_call" | custom-call | tf_op jit(solution)/shard_map/pack_layers/pallas_call | solution.py:435
  2.6 0.5 collective-permute-start.1
  3.1 2.5 %collective-permute-start = (bf16[16,32,512]{2,1,0:T(8,128)(2,1)}, bf16[16,32,512]{2,1,0:T(8,128)(2,1)S(1)}, u32[]{:S(2)}, u32[]{:S(2)}) collective-permute-start(bf16[16,32,512]{2,1,0:T(8,128)(2,1)} %refs_0_), channel_id=1, source_target_pairs={{0,2},{1,3},{2,0},{3,1},{4,6},{5,7},{6,4},{7,5},{8,10},{9,11},{10,... | collective-permute-start | bytes 1572872 | tf_op jit(solution)/shard_map/ppermute | solution.py:447
  5.6 5.8 %all-to-all-start = ((bf16[32,32,128]{2,1,0:T(8,128)(2,1)}), bf16[32,32,128]{2,1,0:T(8,128)(2,1)S(1)}, u32[]{:S(2)}, u32[]{:S(2)}) async-start(bf16[32,32,128]{2,1,0:T(8,128)(2,1)} %pack_layers.1), calls=%async_computation | async-start | bytes 524288 | tf_op jit(solution)/shard_map/all_to_all | solution.py:448
  11.4 0.0 collective-permute-done.1.refs_1_
  11.4 0.0 copy-start
  11.5 0.8 %copy-done = bf16[16,32,512]{2,1,0:T(8,128)(2,1)} copy-done((bf16[16,32,512]{2,1,0:T(8,128)(2,1)}, bf16[16,32,512]{2,1,0:T(8,128)(2,1)S(1)}, u32[]{:S(2)}) %copy-start) | copy-done | bytes 524312
  12.2 6.0 %convolve_near.1 = (f32[16,32,1024]{2,1,0:T(8,128)S(1)}, s32[64]{0:T(128)}, s32[32]{0:T(128)}) custom-call(s32[1]{0:T(128)} %bitcast.me_ref.place_ref, s32[1]{0:T(128)} %bitcast.3.me_ref, s32[1]{0:T(128)S(6)} %copy.13.live_ref, s32[3,2,128]{2,1,0:T(2,128)} %bitcast.5, s32[16,512]{1,0:T(8,128)} %occ.7, bf16[27,32,128]{2,1,0:T(8,128)(2,1)} %weights.5, ...), custom_call_target="tpu_custom_call" | custom-call | tf_op jit(solution)/shard_map/convolve_near/pallas_call | solution.py:459
  18.2 0.2 collective-permute-done.refs_0_
  18.4 0.0 collective-permute-start.2
  18.4 2.3 %all-to-all-done.arrived = bf16[32,32,128]{2,1,0:T(8,128)(2,1)S(1)} async-done(((bf16[32,32,128]{2,1,0:T(8,128)(2,1)}), bf16[32,32,128]{2,1,0:T(8,128)(2,1)S(1)}, u32[]{:S(2)}, u32[]{:S(2)}) %all-to-all-start) | async-done | bytes 262176 | tf_op jit(solution)/shard_map/all_to_all | solution.py:448
  20.7 0.7 %order_layers.1.refs_0_ = bf16[16,32,128]{2,1,0:T(8,128)(2,1)S(1)} custom-call(s32[32]{0:T(128)} %get-tuple-element.27.recv, bf16[32,32,128]{2,1,0:T(8,128)(2,1)S(1)} %all-to-all-done.arrived), custom_call_target="tpu_custom_call" | custom-call | tf_op jit(solution)/shard_map/order_layers/pallas_call | solution.py:476
  21.5 0.1 collective-permute-start.3
  21.5 0.6 collective-permute-start.4
  22.1 1.3 %collective-permute-start.5 = (bf16[16,32,128]{2,1,0:T(8,128)(2,1)S(1)}, bf16[16,32,128]{2,1,0:T(8,128)(2,1)S(1)}, u32[]{:S(2)}, u32[]{:S(2)}) collective-permute-start(bf16[16,32,128]{2,1,0:T(8,128)(2,1)S(1)} %order_layers.1.refs_0_), channel_id=1, source_target_pairs={{0,3},{1,2},{2,1},{3,0},{4,7},{5,6},{6,5},{7,4},{8,11},{9,10},{10,... | collective-permute-start | bytes 393224 | tf_op jit(solution)/shard_map/ppermute | solution.py:410
  23.4 0.0 collective-permute-done.2.refs_1_
  23.4 7.1 %convolve_far.1 = (f32[16,32,1024]{2,1,0:T(8,128)}, f32[16,32,256]{2,1,0:T(8,128)S(1)}, bf16[16,32,384]{2,1,0:T(8,128)(2,1)S(1)}) custom-call(s32[1]{0:T(128)} %bitcast.3.me_ref, s32[1]{0:T(128)S(6)} %copy.13.live_ref, s32[16,512]{1,0:T(8,128)} %occ.7, bf16[27,32,128]{2,1,0:T(8,128)(2,1)} %weights.5, bf16[128,256]{1,0:T(8,128)(2,1)} %constant.19.clone.expand, ...), custom_call_target="tpu_custom_call" | custom-call | tf_op jit(solution)/shard_map/convolve_far/pallas_call | solution.py:487
  30.5 0.0 copy-start.1
  30.5 0.0 collective-permute-done.3.refs_1_
  30.5 0.0 collective-permute-done.4.refs_2_
  30.6 0.0 collective-permute-done.5.refs_3_
  30.6 3.5 %convolve_halo.1 = (f32[16,32,256]{2,1,0:T(8,128)S(1)}, bf16[96,32,128]{2,1,0:T(8,128)(2,1)}) custom-call(s32[1]{0:T(128)} %bitcast.3.me_ref, s32[64]{0:T(128)} %get-tuple-element.32.send, bf16[27,32,128]{2,1,0:T(8,128)(2,1)} %weights.5, bf16[128,256]{1,0:T(8,128)(2,1)} %constant.19.clone.expand, bf16[256,384]{1,0:T(8,128)(2,1)} %constant.23.clone.gather, ...), custom_call_target="tpu_custom_call" | custom-call | tf_op jit(solution)/shard_map/convolve_halo/pallas_call | solution.py:502
  34.1 3.9 %all-to-all-start.1 = ((bf16[96,32,128]{2,1,0:T(8,128)(2,1)}), bf16[96,32,128]{2,1,0:T(8,128)(2,1)S(1)}, u32[]{:S(2)}, u32[]{:S(2)}) async-start(bf16[96,32,128]{2,1,0:T(8,128)(2,1)} %get-tuple-element.36), calls=%async_computation.1 | async-start | bytes 1572864 | tf_op jit(solution)/shard_map/all_to_all | solution.py:525
  38.0 2.8 %late_tables.1.recv = s32[128]{0:T(128)} custom-call(s32[1]{0:T(128)} %bitcast.me_ref.place_ref, s32[3,2,128]{2,1,0:T(2,128)} %bitcast.6), custom_call_target="tpu_custom_call" | custom-call | tf_op jit(solution)/shard_map/late_tables/pallas_call | solution.py:537
  40.8 0.0 copy-done.1
  40.8 0.7 %copy.12.bias = f32[32,1]{1,0:T(8,128)} copy(f32[32,1]{0,1:T(1,128)S(1)} %bitcast.7) | data formatting | bytes 256 | tf_op jit(solution)/shard_map/broadcast_in_dim | solution.py:535
  41.5 4.0 %squeeze_planes.1.base = f32[16,32,512]{2,1,0:T(8,128)S(1)} custom-call(f32[32,1]{1,0:T(8,128)} %copy.12.bias, bf16[256,128]{1,0:T(8,128)(2,1)} %constant.22.clone.squeeze, f32[16,32,1024]{2,1,0:T(8,128)} %get-tuple-element.31.base, f32[16,32,256]{2,1,0:T(8,128)S(1)} %get-tuple-element.35.added), custom_call_target="tpu_custom_call" | custom-call | tf_op jit(solution)/shard_map/squeeze_planes/pallas_call | solution.py:527
  45.4 13.5 %all-to-all-done.1.faces = bf16[96,32,128]{2,1,0:T(8,128)(2,1)S(1)} async-done(((bf16[96,32,128]{2,1,0:T(8,128)(2,1)}), bf16[96,32,128]{2,1,0:T(8,128)(2,1)S(1)}, u32[]{:S(2)}, u32[]{:S(2)}) %all-to-all-start.1) | async-done | bytes 786464 | tf_op jit(solution)/shard_map/all_to_all | solution.py:525
  58.9 2.3 %finish.1 = bf16[16,32,512]{2,1,0:T(8,128)(2,1)} custom-call(s32[128]{0:T(128)} %late_tables.1.recv, s32[1]{0:T(128)S(6)} %copy.13.live_ref, s32[16,512]{1,0:T(8,128)} %occ.7, bf16[384,512]{1,0:T(8,128)(2,1)} %constant.21.clone.scatter, f32[16,32,512]{2,1,0:T(8,128)S(1)} %squeeze_planes.1.base, bf16[96,32,128]{2,1,0:T(8,128)(2,1)S(1)} %all-to-all-done.1.faces), custom_call_target="tpu_custom_call" | custom-call | tf_op jit(solution)/shard_map/finish/pallas_call | solution.py:545
Async XLA Ops:
  2.6 8.8 %collective-permute-start.1 = (bf16[16,32,512]{2,1,0:T(8,128)(2,1)}, bf16[16,32,512]{2,1,0:T(8,128)(2,1)S(1)}, u32[]{:S(2)}, u32[]{:S(2)}) collective-permute-start(bf16[16,32,512]{2,1,0:T(8,128)(2,1)} %refs_0_), channel_id=1, source_target_pairs={{0,1},{1,0},{2,3},{3,2},{4,5},{5,4},{6,7},{7,6},{8,9},{9,8},{10,11... | collective-permute-start | bytes 1572872 | tf_op jit(solution)/shard_map/ppermute | solution.py:404
  3.1 15.3 %collective-permute-start = (bf16[16,32,512]{2,1,0:T(8,128)(2,1)}, bf16[16,32,512]{2,1,0:T(8,128)(2,1)S(1)}, u32[]{:S(2)}, u32[]{:S(2)}) collective-permute-start(bf16[16,32,512]{2,1,0:T(8,128)(2,1)} %refs_0_), channel_id=1, source_target_pairs={{0,2},{1,3},{2,0},{3,1},{4,6},{5,7},{6,4},{7,5},{8,10},{9,11},{10,... | collective-permute-start | bytes 1572872 | tf_op jit(solution)/shard_map/ppermute | solution.py:447
  5.6 15.1 %all-to-all-start = ((bf16[32,32,128]{2,1,0:T(8,128)(2,1)}), bf16[32,32,128]{2,1,0:T(8,128)(2,1)S(1)}, u32[]{:S(2)}, u32[]{:S(2)}) async-start(bf16[32,32,128]{2,1,0:T(8,128)(2,1)} %pack_layers.1), calls=%async_computation | async-start | bytes 524288 | tf_op jit(solution)/shard_map/all_to_all | solution.py:448
  11.4 0.8 %copy-start = (bf16[16,32,512]{2,1,0:T(8,128)(2,1)}, bf16[16,32,512]{2,1,0:T(8,128)(2,1)S(1)}, u32[]{:S(2)}) copy-start(bf16[16,32,512]{2,1,0:T(8,128)(2,1)S(1)} %collective-permute-done.1.refs_1_) | copy-start | bytes 1572868
  18.4 5.0 %collective-permute-start.2 = (bf16[16,32,512]{2,1,0:T(8,128)(2,1)S(1)}, bf16[16,32,512]{2,1,0:T(8,128)(2,1)S(1)}, u32[]{:S(2)}, u32[]{:S(2)}) collective-permute-start(bf16[16,32,512]{2,1,0:T(8,128)(2,1)S(1)} %collective-permute-done.refs_0_), channel_id=1, source_target_pairs={{0,1},{1,0},{2,3},{3,2},{4,5},{5,4},{6,7},{7,6},{8,9},{9,8},{10,11... | collective-permute-start | bytes 1572872 | tf_op jit(solution)/shard_map/ppermute | solution.py:404
  21.5 9.1 %collective-permute-start.3 = (bf16[16,32,128]{2,1,0:T(8,128)(2,1)S(1)}, bf16[16,32,128]{2,1,0:T(8,128)(2,1)S(1)}, u32[]{:S(2)}, u32[]{:S(2)}) collective-permute-start(bf16[16,32,128]{2,1,0:T(8,128)(2,1)S(1)} %order_layers.1.refs_0_), channel_id=1, source_target_pairs={{0,1},{1,0},{2,3},{3,2},{4,5},{5,4},{6,7},{7,6},{8,9},{9,8},{10,11... | collective-permute-start | bytes 393224 | tf_op jit(solution)/shard_map/ppermute | solution.py:410
  21.5 9.0 %collective-permute-start.4 = (bf16[16,32,128]{2,1,0:T(8,128)(2,1)S(1)}, bf16[16,32,128]{2,1,0:T(8,128)(2,1)S(1)}, u32[]{:S(2)}, u32[]{:S(2)}) collective-permute-start(bf16[16,32,128]{2,1,0:T(8,128)(2,1)S(1)} %order_layers.1.refs_0_), channel_id=1, source_target_pairs={{0,2},{1,3},{2,0},{3,1},{4,6},{5,7},{6,4},{7,5},{8,10},{9,11},{10,... | collective-permute-start | bytes 393224 | tf_op jit(solution)/shard_map/ppermute | solution.py:410
  22.1 8.4 %collective-permute-start.5 = (bf16[16,32,128]{2,1,0:T(8,128)(2,1)S(1)}, bf16[16,32,128]{2,1,0:T(8,128)(2,1)S(1)}, u32[]{:S(2)}, u32[]{:S(2)}) collective-permute-start(bf16[16,32,128]{2,1,0:T(8,128)(2,1)S(1)} %order_layers.1.refs_0_), channel_id=1, source_target_pairs={{0,3},{1,2},{2,1},{3,0},{4,7},{5,6},{6,5},{7,4},{8,11},{9,10},{10,... | collective-permute-start | bytes 393224 | tf_op jit(solution)/shard_map/ppermute | solution.py:410
  30.5 10.2 %copy-start.1 = (f32[32]{0:T(128)S(1)}, f32[32]{0:T(128)}, u32[]{:S(2)}) copy-start(f32[32]{0:T(128)} %param.13) | copy-start | bytes 388
  34.1 24.8 %all-to-all-start.1 = ((bf16[96,32,128]{2,1,0:T(8,128)(2,1)}), bf16[96,32,128]{2,1,0:T(8,128)(2,1)S(1)}, u32[]{:S(2)}, u32[]{:S(2)}) async-start(bf16[96,32,128]{2,1,0:T(8,128)(2,1)} %get-tuple-element.36), calls=%async_computation.1 | async-start | bytes 1572864 | tf_op jit(solution)/shard_map/all_to_all | solution.py:525

commit v3 on v2

--- a/solution.py
+++ b/solution.py
@@ -254,11 +254,12 @@
 
 
 def near_kernel(peers, cap, group, place_ref, me_ref, live_ref, nbr, occ, weights, expand, *refs):
-    n = len(refs) - 6 - 3 * group
+    n = len(refs) - 10 - 3 * group
     xs = refs[:n]
-    out, send, recv, wide, count, mask = refs[n : n + 6]
-    sets = [refs[n + 6 + 3 * b : n + 9 + 3 * b] for b in range(group)]
+    out, send, recv, far_wide, halo_wide, far_expand, far_occ, wide, count, mask = refs[n : n + 10]
+    sets = [refs[n + 10 + 3 * b : n + 13 + 3 * b] for b in range(group)]
     me = me_ref[0]
+    channels, every = weights.shape[1:]
     send_slots(peers, cap, group, place_ref, nbr, send, count, True)
     arrival_slots((8, 9), peers, cap, group, place_ref, nbr, recv, mask, True)
     half_weights(weights, wide, div(me, n) == 1)
@@ -266,23 +267,27 @@
     for b, results in enumerate(conv_blocks(blocks, sets, wide, expand)):
         for layer, result in enumerate(results):
             out[b, :, layer * LANES : (layer + 1) * LANES] = result
-
-
-def far_kernel(group, me_ref, live_ref, occ, weights, expand, gather, near, *refs):
-    n = len(refs) - 5 - 3 * group
+    half_weights(weights, far_wide, div(me, n) == 0)
+    for side in range(2):
+        for g in range(3):
+            for r in range(3):
+                halo_wide[side, g * channels : (g + 1) * channels, r * every : (r + 1) * every] = weights[
+                    18 * side + 3 * g + r
+                ]
+    far_expand[...] = expand[...]
+    far_occ[...] = occ[...]
+
+
+def far_kernel(group, me_ref, live_ref, occ, wide, expand, gather, near, *refs):
+    n = len(refs) - 4 - 3 * group
     xs = refs[:n]
-    out, rim, shell = refs[n : n + 3]
-    wide, packed = refs[n + 3 : n + 5]
-    channels = weights.shape[1]
+    out, rim, shell, packed = refs[n : n + 4]
+    channels = near.shape[1]
     step = pl.program_id(0)
     me = me_ref[0]
 
-    @pl.when(step == 0)
-    def _():
-        half_weights(weights, wide, div(me, n) == 0)
-
     blocks = block_parts(group, step, me, live_ref[0], occ, xs)
-    sets = [refs[n + 5 + 3 * b : n + 8 + 3 * b] for b in range(group)]
+    sets = [refs[n + 4 + 3 * b : n + 7 + 3 * b] for b in range(group)]
     for b, results in enumerate(conv_blocks(blocks, sets, wide, expand)):
         for layer, result in enumerate(results):
             at = slice(layer * LANES, (layer + 1) * LANES)
@@ -295,7 +300,7 @@
                 rim[step * group + b, :, side] = total
     picked = jnp.dot(
         packed[...].reshape(group * channels, (SIDE - 2) * LANES),
-        gather[LANES : (SIDE - 1) * LANES, :],
+        gather[...],
         preferred_element_type=jnp.float32,
     )
     shell[pl.ds(step * group, group)] = picked.astype(jnp.bfloat16).reshape(packed.shape[:2] + shell.shape[2:])
@@ -305,19 +310,13 @@
     return jnp.logical_and((lane >> 5) == quarter, ((lane >> 3) & 3) == e)
 
 
-def halo_kernel(slots, cap, me_ref, send, weights, expand, gather, shell, base, *refs):
-    n = len(refs) - 8
+def halo_kernel(slots, cap, me_ref, send, wide, expand, gather, shell, base, *refs):
+    n = len(refs) - 7
     hs = refs[:n]
     added, faces = refs[n : n + 2]
-    wide, rows, stack, prod, packed, edges = refs[n + 2 :]
-    channels, every = weights.shape[1:]
+    rows, stack, prod, packed, edges = refs[n + 2 :]
+    channels, every = wide.shape[1] // 3, wide.shape[2] // 3
     me = me_ref[0]
-    for side in range(2):
-        for g in range(3):
-            for r in range(3):
-                wide[side, g * channels : (g + 1) * channels, r * every : (r + 1) * every] = weights[
-                    18 * side + 3 * g + r
-                ]
     for r in range(slots):
         for key, h in enumerate(hs):
             at = pl.multiple_of((me ^ key) * channels + r * every, channels)
@@ -356,7 +355,9 @@
         faces[peer * size + 2 * cap : (peer + 1) * size] = edges[...]
 
 
-def squeeze_kernel(part, bias, squeeze, base, added, out):
+def squeeze_kernel(part, bias, squeeze, base, added, scatter, occ, out, finish_scatter, finish_occ):
+    finish_scatter[...] = scatter[...]
+    finish_occ[...] = occ[...]
     for n in range(part):
         b = pl.program_id(0) * part + n
         for v in range(4):
@@ -374,26 +375,28 @@
             out[b, :, v * LANES : (v + 1) * LANES] = total
 
 
-def finish_kernel(slots, recv, live_ref, occ, scatter, base, faces, out, shell):
+def finish_kernel(slots, part, recv, live_ref, occ, scatter, base, faces, out, shell):
     channels = base.shape[1]
     live = live_ref[0]
+    first = pl.program_id(0) * part
     lane = lax.broadcasted_iota(jnp.int32, (channels, LANES), 1)
-    for r in range(slots):
+    for n in range(part):
+        r = first + n
         for d in range(2):
             up = faces[recv[2 * d * slots + r]]
             down = faces[recv[(2 * d + 1) * slots + r]]
-            shell[r, :, d * LANES : (d + 1) * LANES] = jnp.where(lane < HALF, down, up)
+            shell[n, :, d * LANES : (d + 1) * LANES] = jnp.where(lane < HALF, down, up)
         total = jnp.zeros((channels, LANES), jnp.bfloat16)
         for e in range(4):
             slot = recv[(4 + e) * slots + r]
             total = jnp.where(edge_mask(lane, slot & 3, e), faces[slot >> 2], total)
-        shell[r, :, 2 * LANES :] = total
+        shell[n, :, 2 * LANES :] = total
     added = jnp.dot(
-        shell[...].reshape(slots * channels, 3 * LANES), scatter[...], preferred_element_type=jnp.float32
+        shell[...].reshape(part * channels, 3 * LANES), scatter[...], preferred_element_type=jnp.float32
     )
-    for r in range(slots):
-        summed = base[r] + added[r * channels : (r + 1) * channels]
-        out[r] = (summed * active_row(occ, r, live)).astype(jnp.bfloat16)
+    for n in range(part):
+        summed = base[first + n] + added[n * channels : (n + 1) * channels]
+        out[n] = (summed * active_row(occ, first + n, live)).astype(jnp.bfloat16)
 
 
 def spread(x, axis, near, size):
@@ -423,9 +426,11 @@
     vmem = pl.BlockSpec(memory_space=pltpu.VMEM)
     resident = lambda x: pltpu.with_memory_space_constraint(x, pltpu.VMEM)
     params = pltpu.CompilerParams(vmem_limit_bytes=VMEM_LIMIT)
-    expand, gather, scatter = (jnp.asarray(t, bf16) for t in tables())
-    squeeze = jnp.asarray(tables()[0].T, bf16)
-    outermost = jnp.asarray(np.concatenate([tables()[1][:LANES], tables()[1][-LANES:]]), bf16)
+    expand, picks, scatter = tables()
+    squeeze, middle, outermost = expand.T, picks[LANES:-LANES], np.concatenate([picks[:LANES], picks[-LANES:]])
+    expand, scatter, squeeze, middle, outermost = (
+        jnp.asarray(t, bf16) for t in (expand, scatter, squeeze, middle, outermost)
+    )
     place = lax.axis_index("blk").astype(i32).reshape(1)
     member = lax.axis_index("ch").astype(i32).reshape(1)
     nbr = neighbours.transpose(1, 2, 0)
@@ -456,15 +461,19 @@
         pltpu.VMEM((9 * channels, SIDE * LANES), f32),
     ] * count
     wide = pltpu.VMEM((9 * channels, 3 * half * channels), bf16)
-    near, send, incoming = pl.pallas_call(
+    near, send, incoming, far_wide, halo_wide, far_expand, far_occ = pl.pallas_call(
         functools.partial(near_kernel, peers, cap, slots),
         out_shape=(
             pltpu.VMEM((slots, channels, SIDE * LANES), f32),
             jax.ShapeDtypeStruct((4 * slots,), i32),
             jax.ShapeDtypeStruct((2 * slots,), i32),
+            pltpu.VMEM((9 * channels, 3 * half * channels), bf16),
+            pltpu.VMEM((2, 3 * channels, 3 * every), bf16),
+            pltpu.VMEM(expand.shape, bf16),
+            pltpu.VMEM(occupancy.shape, i32),
         ),
         in_specs=[smem, smem, smem, smem, vmem, vmem, vmem] + [vmem] * half,
-        out_specs=(vmem, smem, smem),
+        out_specs=(vmem, smem, smem) + (vmem,) * 4,
         scratch_shapes=[wide, pltpu.SMEM((4 * peers,), i32), pltpu.SMEM((2 * peers,), i32)] + buffers(slots),
         compiler_params=params,
         name="convolve_near",
@@ -494,10 +503,16 @@
         ),
         in_specs=[smem, smem, vmem, vmem, vmem, vmem, vmem] + [per_block(voxels)] * half,
         out_specs=(per_block(SIDE * LANES), vmem, vmem),
-        scratch_shapes=[wide, pltpu.VMEM((group, channels, (SIDE - 2) * LANES), bf16)] + buffers(group),
+        scratch_shapes=[
+            pltpu.VMEM((group, channels, (SIDE - 2) * LANES), bf16),
+        ]
+        + buffers(group),
         compiler_params=params,
         name="convolve_far",
-    )(member, live, occupancy, weights, expand, gather, resident(near), *[resident(x) for x in remote])
+    )(
+        member, live, resident(far_occ), resident(far_wide), resident(far_expand), middle, resident(near),
+        *[resident(x) for x in remote],
+    )
 
     added, faces = pl.pallas_call(
         functools.partial(halo_kernel, slots, cap),
@@ -508,7 +523,6 @@
         in_specs=[smem, smem, vmem, vmem, vmem, vmem, vmem] + [vmem] * members,
         out_specs=(vmem, vmem),
         scratch_shapes=[
-            pltpu.VMEM((2, 3 * channels, 3 * every), bf16),
             pltpu.VMEM((slots * every, LANES), bf16),
             pltpu.VMEM((2, 3 * every, slots * LANES), bf16),
             pltpu.VMEM((2, 3 * channels, slots * LANES), f32),
@@ -518,21 +532,25 @@
         compiler_params=params,
         name="convolve_halo",
     )(
-        member, send, weights, expand, outermost, resident(shell), resident(rim),
+        member, send, resident(halo_wide), resident(far_expand), outermost, resident(shell), resident(rim),
         *[resident(x) for x in halo],
     )
 
     faces = lax.all_to_all(faces, "blk", split_axis=0, concat_axis=0, tiled=True)
 
-    base = pl.pallas_call(
+    base, scatter, occupancy = pl.pallas_call(
         functools.partial(squeeze_kernel, part),
         grid=(slots // part,),
-        out_shape=pltpu.VMEM((slots, channels, voxels), f32),
-        in_specs=[vmem, vmem, some(SIDE * LANES), vmem],
-        out_specs=vmem,
+        out_shape=(
+            pltpu.VMEM((slots, channels, voxels), f32),
+            pltpu.VMEM(scatter.shape, bf16),
+            pltpu.VMEM(occupancy.shape, i32),
+        ),
+        in_specs=[vmem, vmem, some(SIDE * LANES), vmem, vmem, vmem],
+        out_specs=(vmem, vmem, vmem),
         compiler_params=params,
         name="squeeze_planes",
-    )(bias[:, None], squeeze, base, resident(added))
+    )(bias[:, None], squeeze, base, resident(added), scatter, occupancy)
 
     recv = pl.pallas_call(
         functools.partial(late_kernel, peers, cap, slots),
@@ -543,15 +561,16 @@
         name="late_tables",
     )(place, nbr)
     return pl.pallas_call(
-        functools.partial(finish_kernel, slots),
+        functools.partial(finish_kernel, slots, group),
+        grid=(slots // group,),
         out_shape=jax.ShapeDtypeStruct((slots, channels, voxels), bf16),
         in_specs=[smem, smem] + [vmem] * 4,
-        out_specs=vmem,
-        scratch_shapes=[pltpu.VMEM((slots, channels, 3 * LANES), bf16)],
+        out_specs=per_block(voxels),
+        scratch_shapes=[pltpu.VMEM((group, channels, 3 * LANES), bf16)],
         compiler_params=params,
         name="finish",
     )(
-        recv, live, occupancy, scatter, resident(base), resident(faces),
+        recv, live, resident(occupancy), resident(scatter), resident(base), resident(faces),
     )
 
 

time: 61.7 us -> 60.6 us (0.982)
  Pallas kernels: 28.3 us -> 27.6 us
    pallas_call x1, Pallas kernels: 7.15 us -> 6.38 us  [shards(): pl.pallas_call(functools.partial(far_kernel, group), grid=(slots // group...]
  transfers between devices with their start and end apart: 8 -> 8, of which waited for: 3 -> 2; matrix products, arithmetic and copies ran while one was open for 1% -> 1% of each run, Pallas kernels for 34% -> 34%
where the time goes in v3:
time: 60.6 us; the launch traced here: 60.1 us
  Pallas kernels  27.6 us (46%)
  waiting for transfers between devices  15.5 us (26%)
  starting transfers between devices  14.7 us (24%)
  local copies, waits for them, and re-layouts  1.48 us (2%)
  between operations  0.75 us (1%)
    all_to_all x1, waiting for transfers between devices, shards(): lax.all_to_all(faces, 'blk', split_axis=0, concat_axis=0, tiled=True)  13.3 us
    pallas_call x1, Pallas kernels, shards(): pl.pallas_call(functools.partial(far_kernel, group), grid=(slots // group...  6.38 us
    pallas_call x1, Pallas kernels, shards(): pl.pallas_call(functools.partial(near_kernel, peers, cap, slots), out_sha...  6.25 us
    all_to_all x1, starting transfers between devices, shards(): lax.all_to_all(outgoing, 'blk', split_axis=0, concat_axis=0, tiled=True)  5.81 us
    pallas_call x1, Pallas kernels, shards(): pl.pallas_call(functools.partial(squeeze_kernel, part), grid=(slots // pa...  4.21 us
    all_to_all x1, starting transfers between devices, shards(): lax.all_to_all(faces, 'blk', split_axis=0, concat_axis=0, tiled=True)  3.91 us
    pallas_call x1, Pallas kernels, shards(): pl.pallas_call(functools.partial(halo_kernel, slots, cap), out_shape=(plt...  3.34 us
    pallas_call x1, Pallas kernels, shards(): pl.pallas_call(functools.partial(late_kernel, peers, cap, slots), out_sha...  2.75 us
  transfers between devices with their start and end apart: 8, of which 2 were waited for; matrix products, arithmetic and copies ran while one was open for 1% of the time, Pallas kernels for 34%

profile of v3, /device:TPU:0, one launch (start us, length us, event | category | flops | bytes accessed | tf_op | source)
XLA Modules:
  0.0 60.1 jit_solution(5349085291601138875)
XLA Ops:
  0.7 2.0 %pack_layers.1 = bf16[32,32,128]{2,1,0:T(8,128)(2,1)} custom-call(s32[1]{0:T(128)} %bitcast.me_ref.place_ref, s32[1]{0:T(128)S(6)} %copy.13.live_ref, s32[3,2,128]{2,1,0:T(2,128)} %bitcast.4, s32[16,512]{1,0:T(8,128)} %occ.5, bf16[16,32,512]{2,1,0:T(8,128)(2,1)} %refs_0_, bf16[16,32,512]{2,1,0:T(8,128)(2,1)} %refs_0_), custom_call_target="tpu_custom_call" | custom-call | tf_op jit(solution)/shard_map/pack_layers/pallas_call | solution.py:440
  2.6 0.5 collective-permute-start
  3.1 2.5 %collective-permute-start.1 = (bf16[16,32,512]{2,1,0:T(8,128)(2,1)}, bf16[16,32,512]{2,1,0:T(8,128)(2,1)S(1)}, u32[]{:S(2)}, u32[]{:S(2)}) collective-permute-start(bf16[16,32,512]{2,1,0:T(8,128)(2,1)} %refs_0_), channel_id=1, source_target_pairs={{0,2},{1,3},{2,0},{3,1},{4,6},{5,7},{6,4},{7,5},{8,10},{9,11},{10,... | collective-permute-start | bytes 1572872 | tf_op jit(solution)/shard_map/ppermute | solution.py:452
  5.6 5.8 %all-to-all-start = ((bf16[32,32,128]{2,1,0:T(8,128)(2,1)}), bf16[32,32,128]{2,1,0:T(8,128)(2,1)S(1)}, u32[]{:S(2)}, u32[]{:S(2)}) async-start(bf16[32,32,128]{2,1,0:T(8,128)(2,1)} %pack_layers.1), calls=%async_computation | async-start | bytes 524288 | tf_op jit(solution)/shard_map/all_to_all | solution.py:453
  11.4 0.0 collective-permute-done.refs_1_
  11.4 0.0 copy-start
  11.4 0.8 %copy-done = bf16[16,32,512]{2,1,0:T(8,128)(2,1)} copy-done((bf16[16,32,512]{2,1,0:T(8,128)(2,1)}, bf16[16,32,512]{2,1,0:T(8,128)(2,1)S(1)}, u32[]{:S(2)}) %copy-start) | copy-done | bytes 524312
  12.2 6.3 %convolve_near.1 = (f32[16,32,1024]{2,1,0:T(8,128)S(1)}, s32[64]{0:T(128)}, s32[32]{0:T(128)}, bf16[288,192]{1,0:T(8,128)(2,1)S(1)}, bf16[2,96,384]{2,1,0:T(8,12...) custom-call(s32[1]{0:T(128)} %bitcast.me_ref.place_ref, s32[1]{0:T(128)} %bitcast.3.me_ref, ...), custom_call_target="tpu_custom_call" | custom-call | tf_op jit(solution)/shard_map/convolve_near/pallas_call | solution.py:464
  18.5 0.0 collective-permute-done.1.refs_0_
  18.5 0.1 collective-permute-start.2
  18.6 2.2 %all-to-all-done.arrived = bf16[32,32,128]{2,1,0:T(8,128)(2,1)S(1)} async-done(((bf16[32,32,128]{2,1,0:T(8,128)(2,1)}), bf16[32,32,128]{2,1,0:T(8,128)(2,1)S(1)}, u32[]{:S(2)}, u32[]{:S(2)}) %all-to-all-start) | async-done | bytes 262176 | tf_op jit(solution)/shard_map/all_to_all | solution.py:453
  20.7 0.7 %order_layers.1.refs_0_ = bf16[16,32,128]{2,1,0:T(8,128)(2,1)S(1)} custom-call(s32[32]{0:T(128)} %get-tuple-element.37.recv, bf16[32,32,128]{2,1,0:T(8,128)(2,1)S(1)} %all-to-all-done.arrived), custom_call_target="tpu_custom_call" | custom-call | tf_op jit(solution)/shard_map/order_layers/pallas_call | solution.py:485
  21.5 0.1 collective-permute-start.3
  21.5 0.6 collective-permute-start.4
  22.1 1.3 %collective-permute-start.5 = (bf16[16,32,128]{2,1,0:T(8,128)(2,1)S(1)}, bf16[16,32,128]{2,1,0:T(8,128)(2,1)S(1)}, u32[]{:S(2)}, u32[]{:S(2)}) collective-permute-start(bf16[16,32,128]{2,1,0:T(8,128)(2,1)S(1)} %order_layers.1.refs_0_), channel_id=1, source_target_pairs={{0,3},{1,2},{2,1},{3,0},{4,7},{5,6},{6,5},{7,4},{8,11},{9,10},{10,... | collective-permute-start | bytes 393224 | tf_op jit(solution)/shard_map/ppermute | solution.py:413
  23.4 0.0 collective-permute-done.2.refs_1_
  23.4 6.4 %convolve_far.1 = (f32[16,32,1024]{2,1,0:T(8,128)}, f32[16,32,256]{2,1,0:T(8,128)S(1)}, bf16[16,32,384]{2,1,0:T(8,128)(2,1)S(1)}) custom-call(s32[1]{0:T(128)} %bitcast.3.me_ref, s32[1]{0:T(128)S(6)} %copy.13.live_ref, s32[16,512]{1,0:T(8,128)S(1)} %get-tuple-element.29.occ, bf16[288,192]{1,0:T(8,128)(2,1)S(1)} %get-tuple-element.30.wide, ...), custom_call_target="tpu_custom_call" | custom-call | tf_op jit(solution)/shard_map/convolve_far/pallas_call | solution.py:496
  29.8 0.0 copy-start.1
  29.8 0.0 collective-permute-done.3.refs_1_
  29.8 0.0 collective-permute-done.4.refs_2_
  29.8 0.0 collective-permute-done.5.refs_3_
  29.8 3.3 %convolve_halo.1 = (f32[16,32,256]{2,1,0:T(8,128)S(1)}, bf16[96,32,128]{2,1,0:T(8,128)(2,1)}) custom-call(s32[1]{0:T(128)} %bitcast.3.me_ref, s32[64]{0:T(128)} %get-tuple-element.42.send, bf16[2,96,384]{2,1,0:T(8,128)(2,1)S(1)} %get-tuple-element.43.wide, bf16[128,256]{1,0:T(8,128)(2,1)S(1)} %get-tuple-element.31.expand, ...), custom_call_target="tpu_custom_call" | custom-call | tf_op jit(solution)/shard_map/convolve_halo/pallas_call | solution.py:517
  33.1 3.9 %all-to-all-start.1 = ((bf16[96,32,128]{2,1,0:T(8,128)(2,1)}), bf16[96,32,128]{2,1,0:T(8,128)(2,1)S(1)}, u32[]{:S(2)}, u32[]{:S(2)}) async-start(bf16[96,32,128]{2,1,0:T(8,128)(2,1)} %get-tuple-element.50), calls=%async_computation.1 | async-start | bytes 1572864 | tf_op jit(solution)/shard_map/all_to_all | solution.py:539
  37.0 2.8 %late_tables.1.recv = s32[128]{0:T(128)} custom-call(s32[1]{0:T(128)} %bitcast.me_ref.place_ref, s32[3,2,128]{2,1,0:T(2,128)} %bitcast.6), custom_call_target="tpu_custom_call" | custom-call | tf_op jit(solution)/shard_map/late_tables/pallas_call | solution.py:555
  39.8 0.0 copy-done.1
  39.8 0.7 %copy.12.bias = f32[32,1]{1,0:T(8,128)} copy(f32[32,1]{0,1:T(1,128)S(1)} %bitcast.7) | data formatting | bytes 256 | tf_op jit(solution)/shard_map/broadcast_in_dim | solution.py:553
  40.5 4.2 %squeeze_planes.1 = (f32[16,32,512]{2,1,0:T(8,128)S(1)}, bf16[384,512]{1,0:T(8,128)(2,1)S(1)}, s32[16,512]{1,0:T(8,128)S(1)}) custom-call(f32[32,1]{1,0:T(8,128)} %copy.12.bias, bf16[256,128]{1,0:T(8,128)(2,1)} %constant.21.clone.squeeze, f32[16,32,1024]{2,1,0:T(8,128)} %get-tuple-element.41.base, f32[16,32,256]{2,1,0:T(8,128)S(1)} %get-tuple-element.46.added, ...), custom_call_target="tpu_custom_call" | custom-call | tf_op jit(solution)/shard_map/squeeze_planes/pallas_call | solution.py:541
  44.7 13.3 %all-to-all-done.1.faces = bf16[96,32,128]{2,1,0:T(8,128)(2,1)S(1)} async-done(((bf16[96,32,128]{2,1,0:T(8,128)(2,1)}), bf16[96,32,128]{2,1,0:T(8,128)(2,1)S(1)}, u32[]{:S(2)}, u32[]{:S(2)}) %all-to-all-start.1) | async-done | bytes 786464 | tf_op jit(solution)/shard_map/all_to_all | solution.py:539
  58.1 2.0 %finish.1 = bf16[16,32,512]{2,1,0:T(8,128)(2,1)} custom-call(s32[128]{0:T(128)} %late_tables.1.recv, s32[1]{0:T(128)S(6)} %copy.13.live_ref, s32[16,512]{1,0:T(8,128)S(1)} %get-tuple-element.47.occ, bf16[384,512]{1,0:T(8,128)(2,1)S(1)} %get-tuple-element.48.scatter, f32[16,32,512]{2,1,0:T(8,128)S(1)} %get-tuple-element.49.base, ...), custom_call_target="tpu_custom_call" | custom-call | tf_op jit(solution)/shard_map/finish/pallas_call | solution.py:563
Async XLA Ops:
  2.6 8.8 %collective-permute-start = (bf16[16,32,512]{2,1,0:T(8,128)(2,1)}, bf16[16,32,512]{2,1,0:T(8,128)(2,1)S(1)}, u32[]{:S(2)}, u32[]{:S(2)}) collective-permute-start(bf16[16,32,512]{2,1,0:T(8,128)(2,1)} %refs_0_), channel_id=1, source_target_pairs={{0,1},{1,0},{2,3},{3,2},{4,5},{5,4},{6,7},{7,6},{8,9},{9,8},{10,11... | collective-permute-start | bytes 1572872 | tf_op jit(solution)/shard_map/ppermute | solution.py:407
  3.1 15.4 %collective-permute-start.1 = (bf16[16,32,512]{2,1,0:T(8,128)(2,1)}, bf16[16,32,512]{2,1,0:T(8,128)(2,1)S(1)}, u32[]{:S(2)}, u32[]{:S(2)}) collective-permute-start(bf16[16,32,512]{2,1,0:T(8,128)(2,1)} %refs_0_), channel_id=1, source_target_pairs={{0,2},{1,3},{2,0},{3,1},{4,6},{5,7},{6,4},{7,5},{8,10},{9,11},{10,... | collective-permute-start | bytes 1572872 | tf_op jit(solution)/shard_map/ppermute | solution.py:452
  5.6 15.1 %all-to-all-start = ((bf16[32,32,128]{2,1,0:T(8,128)(2,1)}), bf16[32,32,128]{2,1,0:T(8,128)(2,1)S(1)}, u32[]{:S(2)}, u32[]{:S(2)}) async-start(bf16[32,32,128]{2,1,0:T(8,128)(2,1)} %pack_layers.1), calls=%async_computation | async-start | bytes 524288 | tf_op jit(solution)/shard_map/all_to_all | solution.py:453
  11.4 0.8 %copy-start = (bf16[16,32,512]{2,1,0:T(8,128)(2,1)}, bf16[16,32,512]{2,1,0:T(8,128)(2,1)S(1)}, u32[]{:S(2)}) copy-start(bf16[16,32,512]{2,1,0:T(8,128)(2,1)S(1)} %collective-permute-done.refs_1_) | copy-start | bytes 1572868
  18.5 4.9 %collective-permute-start.2 = (bf16[16,32,512]{2,1,0:T(8,128)(2,1)S(1)}, bf16[16,32,512]{2,1,0:T(8,128)(2,1)}, u32[]{:S(2)}, u32[]{:S(2)}) collective-permute-start(bf16[16,32,512]{2,1,0:T(8,128)(2,1)S(1)} %collective-permute-done.1.refs_0_), channel_id=1, source_target_pairs={{0,1},{1,0},{2,3},{3,2},{4,5},{5,4},{6,7},{7,6},{8,9},{9,8},{10,11... | collective-permute-start | bytes 1572872 | tf_op jit(solution)/shard_map/ppermute | solution.py:407
  21.5 8.3 %collective-permute-start.3 = (bf16[16,32,128]{2,1,0:T(8,128)(2,1)S(1)}, bf16[16,32,128]{2,1,0:T(8,128)(2,1)S(1)}, u32[]{:S(2)}, u32[]{:S(2)}) collective-permute-start(bf16[16,32,128]{2,1,0:T(8,128)(2,1)S(1)} %order_layers.1.refs_0_), channel_id=1, source_target_pairs={{0,1},{1,0},{2,3},{3,2},{4,5},{5,4},{6,7},{7,6},{8,9},{9,8},{10,11... | collective-permute-start | bytes 393224 | tf_op jit(solution)/shard_map/ppermute | solution.py:413
  21.5 8.2 %collective-permute-start.4 = (bf16[16,32,128]{2,1,0:T(8,128)(2,1)S(1)}, bf16[16,32,128]{2,1,0:T(8,128)(2,1)S(1)}, u32[]{:S(2)}, u32[]{:S(2)}) collective-permute-start(bf16[16,32,128]{2,1,0:T(8,128)(2,1)S(1)} %order_layers.1.refs_0_), channel_id=1, source_target_pairs={{0,2},{1,3},{2,0},{3,1},{4,6},{5,7},{6,4},{7,5},{8,10},{9,11},{10,... | collective-permute-start | bytes 393224 | tf_op jit(solution)/shard_map/ppermute | solution.py:413
  22.1 7.7 %collective-permute-start.5 = (bf16[16,32,128]{2,1,0:T(8,128)(2,1)S(1)}, bf16[16,32,128]{2,1,0:T(8,128)(2,1)S(1)}, u32[]{:S(2)}, u32[]{:S(2)}) collective-permute-start(bf16[16,32,128]{2,1,0:T(8,128)(2,1)S(1)} %order_layers.1.refs_0_), channel_id=1, source_target_pairs={{0,3},{1,2},{2,1},{3,0},{4,7},{5,6},{6,5},{7,4},{8,11},{9,10},{10,... | collective-permute-start | bytes 393224 | tf_op jit(solution)/shard_map/ppermute | solution.py:413
  29.8 10.0 %copy-start.1 = (f32[32]{0:T(128)S(1)}, f32[32]{0:T(128)}, u32[]{:S(2)}) copy-start(f32[32]{0:T(128)} %param.13) | copy-start | bytes 388
  33.1 24.9 %all-to-all-start.1 = ((bf16[96,32,128]{2,1,0:T(8,128)(2,1)}), bf16[96,32,128]{2,1,0:T(8,128)(2,1)S(1)}, u32[]{:S(2)}, u32[]{:S(2)}) async-start(bf16[96,32,128]{2,1,0:T(8,128)(2,1)} %get-tuple-element.50), calls=%async_computation.1 | async-start | bytes 1572864 | tf_op jit(solution)/shard_map/all_to_all | solution.py:539

commit v4 on v3

--- a/solution.py
+++ b/solution.py
@@ -419,7 +419,7 @@
     members = lax.axis_size("ch")
     cap = max(2, 2 * slots // peers)
     every = channels * members
-    group = 8 if slots % 8 == 0 else slots
+    group = slots
     part = 4
     bf16, f32, i32 = jnp.bfloat16, jnp.float32, jnp.int32
     smem = pl.BlockSpec(memory_space=pltpu.SMEM)

time: 60.6 us -> 60.5 us (level)
  no operation moved by 1% of the time
where the time goes in v4:
time: 60.5 us; the launch traced here: 60 us
  Pallas kernels  27.5 us (45%)
  waiting for transfers between devices  15.5 us (26%)
  starting transfers between devices  14.7 us (24%)
  local copies, waits for them, and re-layouts  1.48 us (2%)
  between operations  0.75 us (1%)
    all_to_all x1, waiting for transfers between devices, shards(): lax.all_to_all(faces, 'blk', split_axis=0, concat_axis=0, tiled=True)  13.3 us
    pallas_call x1, Pallas kernels, shards(): pl.pallas_call(functools.partial(far_kernel, group), grid=(slots // group...  6.37 us
    pallas_call x1, Pallas kernels, shards(): pl.pallas_call(functools.partial(near_kernel, peers, cap, slots), out_sha...  6.25 us
    all_to_all x1, starting transfers between devices, shards(): lax.all_to_all(outgoing, 'blk', split_axis=0, concat_axis=0, tiled=True)  5.81 us
    pallas_call x1, Pallas kernels, shards(): pl.pallas_call(functools.partial(squeeze_kernel, part), grid=(slots // pa...  4.21 us
    all_to_all x1, starting transfers between devices, shards(): lax.all_to_all(faces, 'blk', split_axis=0, concat_axis=0, tiled=True)  3.9 us
    pallas_call x1, Pallas kernels, shards(): pl.pallas_call(functools.partial(halo_kernel, slots, cap), out_shape=(plt...  3.34 us
    pallas_call x1, Pallas kernels, shards(): pl.pallas_call(functools.partial(late_kernel, peers, cap, slots), out_sha...  2.75 us
  transfers between devices with their start and end apart: 8, of which 2 were waited for; matrix products, arithmetic and copies ran while one was open for 1% of the time, Pallas kernels for 34%

profile of v4, /device:TPU:0, one launch (start us, length us, event | category | flops | bytes accessed | tf_op | source)
XLA Modules:
  0.0 60.0 jit_solution(5691629828548836634)
XLA Ops:
  0.7 2.0 %pack_layers.1 = bf16[32,32,128]{2,1,0:T(8,128)(2,1)} custom-call(s32[1]{0:T(128)} %bitcast.me_ref.place_ref, s32[1]{0:T(128)S(6)} %copy.13.live_ref, s32[3,2,128]{2,1,0:T(2,128)} %bitcast.4, s32[16,512]{1,0:T(8,128)} %occ.5, bf16[16,32,512]{2,1,0:T(8,128)(2,1)} %refs_0_, bf16[16,32,512]{2,1,0:T(8,128)(2,1)} %refs_0_), custom_call_target="tpu_custom_call" | custom-call | tf_op jit(solution)/shard_map/pack_layers/pallas_call | solution.py:440
  2.6 0.5 collective-permute-start
  3.1 2.5 %collective-permute-start.1 = (bf16[16,32,512]{2,1,0:T(8,128)(2,1)}, bf16[16,32,512]{2,1,0:T(8,128)(2,1)S(1)}, u32[]{:S(2)}, u32[]{:S(2)}) collective-permute-start(bf16[16,32,512]{2,1,0:T(8,128)(2,1)} %refs_0_), channel_id=1, source_target_pairs={{0,2},{1,3},{2,0},{3,1},{4,6},{5,7},{6,4},{7,5},{8,10},{9,11},{10,... | collective-permute-start | bytes 1572872 | tf_op jit(solution)/shard_map/ppermute | solution.py:452
  5.6 5.8 %all-to-all-start = ((bf16[32,32,128]{2,1,0:T(8,128)(2,1)}), bf16[32,32,128]{2,1,0:T(8,128)(2,1)S(1)}, u32[]{:S(2)}, u32[]{:S(2)}) async-start(bf16[32,32,128]{2,1,0:T(8,128)(2,1)} %pack_layers.1), calls=%async_computation | async-start | bytes 524288 | tf_op jit(solution)/shard_map/all_to_all | solution.py:453
  11.4 0.0 collective-permute-done.refs_1_
  11.4 0.0 copy-start
  11.4 0.8 %copy-done = bf16[16,32,512]{2,1,0:T(8,128)(2,1)} copy-done((bf16[16,32,512]{2,1,0:T(8,128)(2,1)}, bf16[16,32,512]{2,1,0:T(8,128)(2,1)S(1)}, u32[]{:S(2)}) %copy-start) | copy-done | bytes 524312
  12.2 6.3 %convolve_near.1 = (f32[16,32,1024]{2,1,0:T(8,128)S(1)}, s32[64]{0:T(128)}, s32[32]{0:T(128)}, bf16[288,192]{1,0:T(8,128)(2,1)S(1)}, bf16[2,96,384]{2,1,0:T(8,12...) custom-call(s32[1]{0:T(128)} %bitcast.me_ref.place_ref, s32[1]{0:T(128)} %bitcast.3.me_ref, ...), custom_call_target="tpu_custom_call" | custom-call | tf_op jit(solution)/shard_map/convolve_near/pallas_call | solution.py:464
  18.5 0.0 collective-permute-done.1.refs_0_
  18.5 0.1 collective-permute-start.2
  18.6 2.2 %all-to-all-done.arrived = bf16[32,32,128]{2,1,0:T(8,128)(2,1)S(1)} async-done(((bf16[32,32,128]{2,1,0:T(8,128)(2,1)}), bf16[32,32,128]{2,1,0:T(8,128)(2,1)S(1)}, u32[]{:S(2)}, u32[]{:S(2)}) %all-to-all-start) | async-done | bytes 262176 | tf_op jit(solution)/shard_map/all_to_all | solution.py:453
  20.7 0.7 %order_layers.1.refs_0_ = bf16[16,32,128]{2,1,0:T(8,128)(2,1)S(1)} custom-call(s32[32]{0:T(128)} %get-tuple-element.37.recv, bf16[32,32,128]{2,1,0:T(8,128)(2,1)S(1)} %all-to-all-done.arrived), custom_call_target="tpu_custom_call" | custom-call | tf_op jit(solution)/shard_map/order_layers/pallas_call | solution.py:485
  21.5 0.1 collective-permute-start.3
  21.5 0.6 collective-permute-start.4
  22.1 1.3 %collective-permute-start.5 = (bf16[16,32,128]{2,1,0:T(8,128)(2,1)S(1)}, bf16[16,32,128]{2,1,0:T(8,128)(2,1)S(1)}, u32[]{:S(2)}, u32[]{:S(2)}) collective-permute-start(bf16[16,32,128]{2,1,0:T(8,128)(2,1)S(1)} %order_layers.1.refs_0_), channel_id=1, source_target_pairs={{0,3},{1,2},{2,1},{3,0},{4,7},{5,6},{6,5},{7,4},{8,11},{9,10},{10,... | collective-permute-start | bytes 393224 | tf_op jit(solution)/shard_map/ppermute | solution.py:413
  23.4 0.0 collective-permute-done.2.refs_1_
  23.4 6.4 %convolve_far.1 = (f32[16,32,1024]{2,1,0:T(8,128)}, f32[16,32,256]{2,1,0:T(8,128)S(1)}, bf16[16,32,384]{2,1,0:T(8,128)(2,1)S(1)}) custom-call(s32[1]{0:T(128)} %bitcast.3.me_ref, s32[1]{0:T(128)S(6)} %copy.13.live_ref, s32[16,512]{1,0:T(8,128)S(1)} %get-tuple-element.29.occ, bf16[288,192]{1,0:T(8,128)(2,1)S(1)} %get-tuple-element.30.wide, ...), custom_call_target="tpu_custom_call" | custom-call | tf_op jit(solution)/shard_map/convolve_far/pallas_call | solution.py:496
  29.8 0.0 copy-start.1
  29.8 0.0 collective-permute-done.3.refs_1_
  29.8 0.0 collective-permute-done.4.refs_2_
  29.8 0.0 collective-permute-done.5.refs_3_
  29.8 3.3 %convolve_halo.1 = (f32[16,32,256]{2,1,0:T(8,128)S(1)}, bf16[96,32,128]{2,1,0:T(8,128)(2,1)}) custom-call(s32[1]{0:T(128)} %bitcast.3.me_ref, s32[64]{0:T(128)} %get-tuple-element.42.send, bf16[2,96,384]{2,1,0:T(8,128)(2,1)S(1)} %get-tuple-element.43.wide, bf16[128,256]{1,0:T(8,128)(2,1)S(1)} %get-tuple-element.31.expand, ...), custom_call_target="tpu_custom_call" | custom-call | tf_op jit(solution)/shard_map/convolve_halo/pallas_call | solution.py:517
  33.1 3.9 %all-to-all-start.1 = ((bf16[96,32,128]{2,1,0:T(8,128)(2,1)}), bf16[96,32,128]{2,1,0:T(8,128)(2,1)S(1)}, u32[]{:S(2)}, u32[]{:S(2)}) async-start(bf16[96,32,128]{2,1,0:T(8,128)(2,1)} %get-tuple-element.50), calls=%async_computation.1 | async-start | bytes 1572864 | tf_op jit(solution)/shard_map/all_to_all | solution.py:539
  37.0 2.8 %late_tables.1.recv = s32[128]{0:T(128)} custom-call(s32[1]{0:T(128)} %bitcast.me_ref.place_ref, s32[3,2,128]{2,1,0:T(2,128)} %bitcast.6), custom_call_target="tpu_custom_call" | custom-call | tf_op jit(solution)/shard_map/late_tables/pallas_call | solution.py:555
  39.8 0.0 copy-done.1
  39.8 0.7 %copy.12.bias = f32[32,1]{1,0:T(8,128)} copy(f32[32,1]{0,1:T(1,128)S(1)} %bitcast.7) | data formatting | bytes 256 | tf_op jit(solution)/shard_map/broadcast_in_dim | solution.py:553
  40.5 4.2 %squeeze_planes.1 = (f32[16,32,512]{2,1,0:T(8,128)S(1)}, bf16[384,512]{1,0:T(8,128)(2,1)S(1)}, s32[16,512]{1,0:T(8,128)S(1)}) custom-call(f32[32,1]{1,0:T(8,128)} %copy.12.bias, bf16[256,128]{1,0:T(8,128)(2,1)} %constant.21.clone.squeeze, f32[16,32,1024]{2,1,0:T(8,128)} %get-tuple-element.41.base, f32[16,32,256]{2,1,0:T(8,128)S(1)} %get-tuple-element.46.added, ...), custom_call_target="tpu_custom_call" | custom-call | tf_op jit(solution)/shard_map/squeeze_planes/pallas_call | solution.py:541
  44.7 13.3 %all-to-all-done.1.faces = bf16[96,32,128]{2,1,0:T(8,128)(2,1)S(1)} async-done(((bf16[96,32,128]{2,1,0:T(8,128)(2,1)}), bf16[96,32,128]{2,1,0:T(8,128)(2,1)S(1)}, u32[]{:S(2)}, u32[]{:S(2)}) %all-to-all-start.1) | async-done | bytes 786464 | tf_op jit(solution)/shard_map/all_to_all | solution.py:539
  58.1 1.9 %finish.1 = bf16[16,32,512]{2,1,0:T(8,128)(2,1)} custom-call(s32[128]{0:T(128)} %late_tables.1.recv, s32[1]{0:T(128)S(6)} %copy.13.live_ref, s32[16,512]{1,0:T(8,128)S(1)} %get-tuple-element.47.occ, bf16[384,512]{1,0:T(8,128)(2,1)S(1)} %get-tuple-element.48.scatter, f32[16,32,512]{2,1,0:T(8,128)S(1)} %get-tuple-element.49.base, ...), custom_call_target="tpu_custom_call" | custom-call | tf_op jit(solution)/shard_map/finish/pallas_call | solution.py:563
Async XLA Ops:
  2.6 8.8 %collective-permute-start = (bf16[16,32,512]{2,1,0:T(8,128)(2,1)}, bf16[16,32,512]{2,1,0:T(8,128)(2,1)S(1)}, u32[]{:S(2)}, u32[]{:S(2)}) collective-permute-start(bf16[16,32,512]{2,1,0:T(8,128)(2,1)} %refs_0_), channel_id=1, source_target_pairs={{0,1},{1,0},{2,3},{3,2},{4,5},{5,4},{6,7},{7,6},{8,9},{9,8},{10,11... | collective-permute-start | bytes 1572872 | tf_op jit(solution)/shard_map/ppermute | solution.py:407
  3.1 15.4 %collective-permute-start.1 = (bf16[16,32,512]{2,1,0:T(8,128)(2,1)}, bf16[16,32,512]{2,1,0:T(8,128)(2,1)S(1)}, u32[]{:S(2)}, u32[]{:S(2)}) collective-permute-start(bf16[16,32,512]{2,1,0:T(8,128)(2,1)} %refs_0_), channel_id=1, source_target_pairs={{0,2},{1,3},{2,0},{3,1},{4,6},{5,7},{6,4},{7,5},{8,10},{9,11},{10,... | collective-permute-start | bytes 1572872 | tf_op jit(solution)/shard_map/ppermute | solution.py:452
  5.6 15.1 %all-to-all-start = ((bf16[32,32,128]{2,1,0:T(8,128)(2,1)}), bf16[32,32,128]{2,1,0:T(8,128)(2,1)S(1)}, u32[]{:S(2)}, u32[]{:S(2)}) async-start(bf16[32,32,128]{2,1,0:T(8,128)(2,1)} %pack_layers.1), calls=%async_computation | async-start | bytes 524288 | tf_op jit(solution)/shard_map/all_to_all | solution.py:453
  11.4 0.8 %copy-start = (bf16[16,32,512]{2,1,0:T(8,128)(2,1)}, bf16[16,32,512]{2,1,0:T(8,128)(2,1)S(1)}, u32[]{:S(2)}) copy-start(bf16[16,32,512]{2,1,0:T(8,128)(2,1)S(1)} %collective-permute-done.refs_1_) | copy-start | bytes 1572868
  18.5 4.9 %collective-permute-start.2 = (bf16[16,32,512]{2,1,0:T(8,128)(2,1)S(1)}, bf16[16,32,512]{2,1,0:T(8,128)(2,1)}, u32[]{:S(2)}, u32[]{:S(2)}) collective-permute-start(bf16[16,32,512]{2,1,0:T(8,128)(2,1)S(1)} %collective-permute-done.1.refs_0_), channel_id=1, source_target_pairs={{0,1},{1,0},{2,3},{3,2},{4,5},{5,4},{6,7},{7,6},{8,9},{9,8},{10,11... | collective-permute-start | bytes 1572872 | tf_op jit(solution)/shard_map/ppermute | solution.py:407
  21.5 8.3 %collective-permute-start.3 = (bf16[16,32,128]{2,1,0:T(8,128)(2,1)S(1)}, bf16[16,32,128]{2,1,0:T(8,128)(2,1)S(1)}, u32[]{:S(2)}, u32[]{:S(2)}) collective-permute-start(bf16[16,32,128]{2,1,0:T(8,128)(2,1)S(1)} %order_layers.1.refs_0_), channel_id=1, source_target_pairs={{0,1},{1,0},{2,3},{3,2},{4,5},{5,4},{6,7},{7,6},{8,9},{9,8},{10,11... | collective-permute-start | bytes 393224 | tf_op jit(solution)/shard_map/ppermute | solution.py:413
  21.5 8.2 %collective-permute-start.4 = (bf16[16,32,128]{2,1,0:T(8,128)(2,1)S(1)}, bf16[16,32,128]{2,1,0:T(8,128)(2,1)S(1)}, u32[]{:S(2)}, u32[]{:S(2)}) collective-permute-start(bf16[16,32,128]{2,1,0:T(8,128)(2,1)S(1)} %order_layers.1.refs_0_), channel_id=1, source_target_pairs={{0,2},{1,3},{2,0},{3,1},{4,6},{5,7},{6,4},{7,5},{8,10},{9,11},{10,... | collective-permute-start | bytes 393224 | tf_op jit(solution)/shard_map/ppermute | solution.py:413
  22.1 7.7 %collective-permute-start.5 = (bf16[16,32,128]{2,1,0:T(8,128)(2,1)S(1)}, bf16[16,32,128]{2,1,0:T(8,128)(2,1)S(1)}, u32[]{:S(2)}, u32[]{:S(2)}) collective-permute-start(bf16[16,32,128]{2,1,0:T(8,128)(2,1)S(1)} %order_layers.1.refs_0_), channel_id=1, source_target_pairs={{0,3},{1,2},{2,1},{3,0},{4,7},{5,6},{6,5},{7,4},{8,11},{9,10},{10,... | collective-permute-start | bytes 393224 | tf_op jit(solution)/shard_map/ppermute | solution.py:413
  29.8 10.0 %copy-start.1 = (f32[32]{0:T(128)S(1)}, f32[32]{0:T(128)}, u32[]{:S(2)}) copy-start(f32[32]{0:T(128)} %param.13) | copy-start | bytes 388
  33.1 24.9 %all-to-all-start.1 = ((bf16[96,32,128]{2,1,0:T(8,128)(2,1)}), bf16[96,32,128]{2,1,0:T(8,128)(2,1)S(1)}, u32[]{:S(2)}, u32[]{:S(2)}) async-start(bf16[96,32,128]{2,1,0:T(8,128)(2,1)} %get-tuple-element.50), calls=%async_computation.1 | async-start | bytes 1572864 | tf_op jit(solution)/shard_map/all_to_all | solution.py:539
